TPU v7x, 256 devices: a whole 4x4x8 slice. The times are simulated.
256 devices in a mesh: lon: 8 (over y_hi, x), lat: 32 (over z, y_lo, core).
Axes of the slice: x: 4, y: 4 (y_hi: 2, y_lo: 2; y = y_hi * 2 + y_lo), z: 8, core: 2. Of those that a mesh axis runs over, the one named last changes fastest.
Arguments:
- prognostic: bfloat16 [7, 8, 512, 4096], P(None, None, 'lat', 'lon'), may hold values from -6 to 6
- halo_depth: int32 [2, 32, 8], P(None, 'lat', 'lon'), may hold values from 3 to 10, as said below
- cell_offsets: int32 [2, 8, 512, 4096], P(None, None, 'lat', 'lon'), may hold values from -8 to 8, as said below
Outputs:
- advected: bfloat16 [7, 8, 512, 4096], P(None, None, 'lat', 'lon')
Inputs may be any that keep to these rules, and one draw needn't show every extreme that they name: `halo_depth`: every depth is 3 or more; row depths are at most 10, column depths at most 8; some tile has row depth 10 and column depth 8. |cell_offsets[0]| <= (its tile's row depth) - 2 and |cell_offsets[1]| <= (its tile's column depth) - 2; row y + cell_offsets[0] lies in 0 to 510.
All inputs are finite; a program needn't handle non-finite values.
Results may differ from a plain program's by a relative error of at most 0.0047.
Values may be sent and summed in bfloat16 or wider, within the bound.
No kernel may reach another device: no remote copies, remote signals or barrier semaphores. Data moves between devices by JAX's collectives and lax.ppermute only.
A program may use at most 64 MiB of HBM per device.

v0:
```python
import math

import jax
import jax.numpy as jnp
from jax import lax
from jax.sharding import PartitionSpec as P

HO = 8
HL = 10
ITERS = 3


courant = 2.0


def passed_along(value, axis, by):
    devices = lax.axis_size(axis)
    pairs = [(i, i + by) for i in range(devices) if 0 <= i + by < devices]
    return lax.ppermute(value, axis, pairs)


def from_behind(value, axis, steps):
    count = lax.axis_size(axis)
    pairs = [(source, (source + steps) % count) for source in range(count)]
    return lax.ppermute(value, axis, pairs)


def keys_kernel(offset):
    magnitude = jnp.abs(offset)
    near_part = (1.5 * magnitude - 2.5) * magnitude * magnitude + 1.0
    far_part = ((-0.5 * magnitude + 2.5) * magnitude - 4.0) * magnitude + 2.0
    return jnp.where(magnitude <= 1.0, near_part, jnp.where(magnitude < 2.0, far_part, 0.0))


def band_sample(extended, row_off, row_frac, col_off, col_frac, row_first, row_span, halo_rows):
    channels = extended.shape[0]
    lat_count, lon_count = row_off.shape
    block_width = min(128, lon_count)
    block_count = lon_count // block_width
    band_width = block_width + 2 * HO
    pieces = lat_count * block_count
    windows = []
    for row_index in range(lat_count):
        for block_index in range(block_count):
            first_col = block_index * block_width
            windows.append(
                extended[
                    :,
                    row_index + row_first : row_index + row_first + row_span,
                    first_col : first_col + band_width,
                ]
            )
    windows = jnp.stack(windows)
    col_start = col_off.reshape(pieces, block_width)
    col_part = col_frac.reshape(pieces, block_width)
    row_start = row_off.reshape(pieces, block_width)
    row_part = row_frac.reshape(pieces, block_width)
    col_rel = (
        jnp.arange(band_width, dtype=jnp.int32)[None, None, :]
        - HO
        - jnp.arange(block_width, dtype=jnp.int32)[None, :, None]
    )
    band_weight = keys_kernel(
        (col_rel - col_start[:, :, None]).astype(jnp.float32) - col_part[:, :, None]
    ).astype(jnp.bfloat16)
    row_rel = jnp.arange(row_span, dtype=jnp.int32)[None, :, None] + (row_first - halo_rows)
    row_weight = keys_kernel(
        (row_rel - row_start[:, None, :]).astype(jnp.float32) - row_part[:, None, :]
    )
    lon_mixed = jnp.einsum(
        "ncrw,niw->ncri", windows, band_weight, preferred_element_type=jnp.float32
    )
    summed = jnp.sum(lon_mixed * row_weight[:, None, :, :], axis=2)
    summed = summed.reshape(lat_count, block_count, channels, block_width)
    return jnp.transpose(summed, (2, 0, 1, 3)).reshape(channels, lat_count, lon_count)


def lat_wrap(fields):
    from_lower = passed_along(fields[:, :, fields.shape[2] - HL :], "lat", 1)
    from_upper = passed_along(fields[:, :, :HL], "lat", -1)
    return jnp.concatenate([from_lower, fields, from_upper], axis=2)


def lon_wrap(fields):
    channels, levels, row_count, col_count = fields.shape
    west_edge = jnp.moveaxis(fields[:, :, :, :HO], 3, 0).reshape(HO, channels * levels * row_count)
    east_edge = jnp.moveaxis(fields[:, :, :, col_count - HO :], 3, 0).reshape(
        HO, channels * levels * row_count
    )
    west_cols = from_behind(east_edge, "lon", 1)
    east_cols = from_behind(west_edge, "lon", -1)
    west_cols = jnp.moveaxis(west_cols.reshape(HO, channels, levels, row_count), 0, 3)
    east_cols = jnp.moveaxis(east_cols.reshape(HO, channels, levels, row_count), 0, 3)
    return jnp.concatenate([west_cols, fields, east_cols], axis=3)


def extend(fields):
    return lon_wrap(lat_wrap(fields))


def on_device(prognostic, halo_depth, cell_offsets):
    channels, levels, lat_count, lon_count = prognostic.shape
    halo_rows = HL
    whole_ext = extend(prognostic)
    wind_ext = whole_ext[0:2]
    lat_total = lat_count * lax.axis_size("lat")
    lat_index = (lax.axis_index("lat") * lat_count + jnp.arange(lat_count, dtype=jnp.int32)).astype(
        jnp.float32
    )
    coslat = jnp.cos((lat_index + 0.5) * (math.pi / lat_total) - 0.5 * math.pi)[:, None]
    rows_depth = halo_depth[0, 0, 0].astype(jnp.float32)
    cols_depth = halo_depth[1, 0, 0].astype(jnp.float32)

    def track_level(level_index):
        wind_level = lax.dynamic_index_in_dim(wind_ext, level_index, 1, keepdims=False)
        offsets_level = lax.dynamic_index_in_dim(cell_offsets, level_index, 1, keepdims=False)
        row_off = offsets_level[0]
        col_off = offsets_level[1]
        row_frac = jnp.full(row_off.shape, 0.5, jnp.float32)
        col_frac = jnp.full(col_off.shape, 0.5, jnp.float32)
        row_mid = jnp.floor_divide(row_off, 2)
        col_mid = jnp.floor_divide(col_off, 2)
        row_float = row_off.astype(jnp.float32)
        col_float = col_off.astype(jnp.float32)
        for repeat in range(ITERS):
            row_part = ((row_off - 2 * row_mid).astype(jnp.float32) + row_frac) * 0.5
            col_part = ((col_off - 2 * col_mid).astype(jnp.float32) + col_frac) * 0.5
            mid_wind = band_sample(
                wind_level,
                row_mid,
                row_part,
                col_mid,
                col_part,
                halo_rows // 2,
                halo_rows + 2,
                halo_rows,
            )
            lon_reach = -courant * mid_wind[0] / coslat
            lat_reach = -courant * mid_wind[1]
            lon_limit = (cols_depth - 1.0) * jnp.tanh(lon_reach / (cols_depth - 1.0))
            lat_limit = (rows_depth - 1.0) * jnp.tanh(lat_reach / (rows_depth - 1.0))
            row_frac = 0.5 + 0.5 * jnp.tanh(0.5 * (lat_limit - row_float - 0.5))
            col_frac = 0.5 + 0.5 * jnp.tanh(0.5 * (lon_limit - col_float - 0.5))
        return (row_frac, col_frac)

    row_fracs, col_fracs = lax.map(track_level, jnp.arange(levels, dtype=jnp.int32))

    def advect_level(level_index):
        fields_level = lax.dynamic_index_in_dim(whole_ext, level_index, 1, keepdims=False)
        offsets_level = lax.dynamic_index_in_dim(cell_offsets, level_index, 1, keepdims=False)
        row_frac = lax.dynamic_index_in_dim(row_fracs, level_index, 0, keepdims=False)
        col_frac = lax.dynamic_index_in_dim(col_fracs, level_index, 0, keepdims=False)
        sampled = band_sample(
            fields_level,
            offsets_level[0],
            row_frac,
            offsets_level[1],
            col_frac,
            1,
            2 * halo_rows,
            halo_rows,
        )
        return sampled.astype(jnp.bfloat16)

    advected = lax.map(advect_level, jnp.arange(levels, dtype=jnp.int32))
    return jnp.moveaxis(advected, 0, 1)


def solution(mesh):
    in_specs = (P(None, None, "lat", "lon"), P(None, "lat", "lon"), P(None, None, "lat", "lon"))
    out_specs = P(None, None, "lat", "lon")
    return jax.shard_map(
        on_device, mesh=mesh, in_specs=in_specs, out_specs=out_specs, check_vma=False
    )
```

profile of v0, /device:TPU:135, one launch (start us, length us, event | category | flops | bytes accessed | tf_op | source)
XLA Modules:
  0.0 358.5 jit_solution(13373083182122507743)
XLA Ops:
  2.3 3.8 %collective-permute-start = (bf16[7,8,10,512]{3,1,2,0:T(8,128)(2,1)S(1)}, bf16[7,8,10,512]{3,1,2,0:T(8,128)(2,1)S(1)}, u32[]{:S(2)}, u32[]{:S(2)}) collective-permute-start(bf16[7,8,10,512]{3,1,2,0:T(8,128)(2,1)S(1)} %copy.79), channel_id=1, source_target_pairs={{0,1},{1,2},{2,3},{3,4},{4,5},{5,6},{6,7},{7,8},{8,9},{9,10},{10,1... | collective-permute-start | bytes 1720328 | tf_op jit(solution)/shard_map/ppermute | solution.py:19
  8.3 10.5 %collective-permute-done = bf16[7,8,10,512]{3,1,2,0:T(8,128)(2,1)S(1)} collective-permute-done((bf16[7,8,10,512]{3,1,2,0:T(8,128)(2,1)S(1)}, bf16[7,8,10,512]{3,1,2,0:T(8,128)(2,1)S(1)}, u32[]{:S(2)}, u32[]{:S(2)}) %collective-permute-start) | collective-permute-done | bytes 573472 | tf_op jit(solution)/shard_map/ppermute | solution.py:19
  30.9 3.9 %collective-permute-done.3 = bf16[8,2016]{1,0:T(8,128)(2,1)} collective-permute-done((bf16[8,2016]{1,0:T(8,128)(2,1)S(1)}, bf16[8,2016]{1,0:T(8,128)(2,1)}, u32[]{:S(2)}, u32[]{:S(2)}) %collective-permute-start.3) | collective-permute-done | bytes 32288 | tf_op jit(solution)/shard_map/ppermute | solution.py:25
  37.0 5.3 %pad_maximum_fusion = bf16[7,8,36,528]{3,2,0,1:T(8,128)(2,1)} fusion(bf16[7,8,36,8]{3,2,0,1:T(8,128)(2,1)} %copy.59, bf16[7,8,10,512]{3,2,0,1:T(8,128)(2,1)S(1)} %copy.55, bf16[7,8,10,512]{3,2,0,1:T(8,128)(2,1)S(1)} %copy.53, bf16[7,8,36,8]{3,2,0,1:T(8,128)(2,1)S(1)} %copy.58, bf16[7,8,16,512]{3,2,1,0:T(8,128)(2,1)S(1)} %copy-done), kind=kLoop, calls=%fused_computation.464 | loop fusion | flops 10644480 | bytes 4257792 | tf_op jit(solution)/shard_map/concatenate | solution.py:94
  43.5 168.7 %while.30 = (s32[]{:T(128)}, f32[8,16,512]{2,0,1:T(8,128)}, f32[8,16,512]{2,0,1:T(8,128)}, f32[]{:T(128)}, s32[8]{0:T(128)S(1)}, /*index=5*/bf16[2,8,36,528]{3,2...) while((s32[]{:T(128)}, f32[8,16,512]{2,0,1:T(8,128)}, ...), condition=%wide.region_4.5_spmd.clone, body=%wide.region_0.4_spmd.clone.sunk | while | flops 249071872 | bytes 9238763 | solution.py:146
  48.4 3.6 %fusion.198 = f32[64,2,128]{2,1,0:T(2,128)S(1)} fusion(bf16[64,2,12,144]{3,2,1,0:T(8,128)(2,1)S(1)} %constant_dynamic-update-slice_fusion.383, f32[64,128]{1,0:T(8,128)S(1)} %add_multiply_fusion.12, s32[64,128]{1,0:T(8,128)S(1)} %add_select_fusion.4, s32[128,144]{0,1:T(8,128)S(1)} %iota_subtract_fusion.5, f32[64,12,128]{2,1,0:T(8,128)S(1)} %fusion.197), kind=kOutput, calls=%fused_computation.235.clone.1 | convolution fusion | flops 80592896 | bytes 1040384 | tf_op jit(solution)/shard_map/while/body/eval_jaxpr/ncrw,niw->ncri/dot_general | solution.py:70
  52.9 3.6 %fusion.202 = f32[64,2,128]{2,1,0:T(2,128)S(1)} fusion(bf16[64,2,12,144]{3,2,1,0:T(8,128)(2,1)S(1)} %constant_dynamic-update-slice_fusion.383, f32[64,128]{1,0:T(8,128)S(1)} %add_multiply_fusion.14, s32[64,128]{1,0:T(8,128)S(1)} %add_select_fusion.4, s32[128,144]{0,1:T(8,128)S(1)} %iota_subtract_fusion.5, f32[64,12,128]{2,1,0:T(8,128)S(1)} %fusion.201), kind=kOutput, calls=%fused_computation.236.clone.1 | convolution fusion | flops 80592896 | bytes 1040384 | tf_op jit(solution)/shard_map/while/body/eval_jaxpr/ncrw,niw->ncri/dot_general | solution.py:70
  57.2 3.6 %fusion.205 = f32[64,2,128]{2,1,0:T(2,128)S(1)} fusion(bf16[64,2,12,144]{3,2,1,0:T(8,128)(2,1)S(1)} %constant_dynamic-update-slice_fusion.383, f32[64,128]{1,0:T(8,128)S(1)} %add_multiply_fusion.16, s32[64,128]{1,0:T(8,128)S(1)} %add_select_fusion.4, s32[128,144]{0,1:T(8,128)S(1)} %iota_subtract_fusion.5, f32[64,12,128]{2,1,0:T(8,128)S(1)} %fusion.204), kind=kOutput, calls=%fused_computation.237.clone.1 | convolution fusion | flops 80592896 | bytes 1040384 | tf_op jit(solution)/shard_map/while/body/eval_jaxpr/ncrw,niw->ncri/dot_general | solution.py:70
  69.5 3.6 %fusion.198 = f32[64,2,128]{2,1,0:T(2,128)S(1)} fusion(bf16[64,2,12,144]{3,2,1,0:T(8,128)(2,1)S(1)} %constant_dynamic-update-slice_fusion.383, f32[64,128]{1,0:T(8,128)S(1)} %add_multiply_fusion.12, s32[64,128]{1,0:T(8,128)S(1)} %add_select_fusion.4, s32[128,144]{0,1:T(8,128)S(1)} %iota_subtract_fusion.5, f32[64,12,128]{2,1,0:T(8,128)S(1)} %fusion.197), kind=kOutput, calls=%fused_computation.235.clone.1 | convolution fusion | flops 80592896 | bytes 1040384 | tf_op jit(solution)/shard_map/while/body/eval_jaxpr/ncrw,niw->ncri/dot_general | solution.py:70
  74.0 3.6 %fusion.202 = f32[64,2,128]{2,1,0:T(2,128)S(1)} fusion(bf16[64,2,12,144]{3,2,1,0:T(8,128)(2,1)S(1)} %constant_dynamic-update-slice_fusion.383, f32[64,128]{1,0:T(8,128)S(1)} %add_multiply_fusion.14, s32[64,128]{1,0:T(8,128)S(1)} %add_select_fusion.4, s32[128,144]{0,1:T(8,128)S(1)} %iota_subtract_fusion.5, f32[64,12,128]{2,1,0:T(8,128)S(1)} %fusion.201), kind=kOutput, calls=%fused_computation.236.clone.1 | convolution fusion | flops 80592896 | bytes 1040384 | tf_op jit(solution)/shard_map/while/body/eval_jaxpr/ncrw,niw->ncri/dot_general | solution.py:70
  78.2 3.6 %fusion.205 = f32[64,2,128]{2,1,0:T(2,128)S(1)} fusion(bf16[64,2,12,144]{3,2,1,0:T(8,128)(2,1)S(1)} %constant_dynamic-update-slice_fusion.383, f32[64,128]{1,0:T(8,128)S(1)} %add_multiply_fusion.16, s32[64,128]{1,0:T(8,128)S(1)} %add_select_fusion.4, s32[128,144]{0,1:T(8,128)S(1)} %iota_subtract_fusion.5, f32[64,12,128]{2,1,0:T(8,128)S(1)} %fusion.204), kind=kOutput, calls=%fused_computation.237.clone.1 | convolution fusion | flops 80592896 | bytes 1040384 | tf_op jit(solution)/shard_map/while/body/eval_jaxpr/ncrw,niw->ncri/dot_general | solution.py:70
  90.6 3.6 %fusion.198 = f32[64,2,128]{2,1,0:T(2,128)S(1)} fusion(bf16[64,2,12,144]{3,2,1,0:T(8,128)(2,1)S(1)} %constant_dynamic-update-slice_fusion.383, f32[64,128]{1,0:T(8,128)S(1)} %add_multiply_fusion.12, s32[64,128]{1,0:T(8,128)S(1)} %add_select_fusion.4, s32[128,144]{0,1:T(8,128)S(1)} %iota_subtract_fusion.5, f32[64,12,128]{2,1,0:T(8,128)S(1)} %fusion.197), kind=kOutput, calls=%fused_computation.235.clone.1 | convolution fusion | flops 80592896 | bytes 1040384 | tf_op jit(solution)/shard_map/while/body/eval_jaxpr/ncrw,niw->ncri/dot_general | solution.py:70
  99.3 3.6 %fusion.205 = f32[64,2,128]{2,1,0:T(2,128)S(1)} fusion(bf16[64,2,12,144]{3,2,1,0:T(8,128)(2,1)S(1)} %constant_dynamic-update-slice_fusion.383, f32[64,128]{1,0:T(8,128)S(1)} %add_multiply_fusion.16, s32[64,128]{1,0:T(8,128)S(1)} %add_select_fusion.4, s32[128,144]{0,1:T(8,128)S(1)} %iota_subtract_fusion.5, f32[64,12,128]{2,1,0:T(8,128)S(1)} %fusion.204), kind=kOutput, calls=%fused_computation.237.clone.1 | convolution fusion | flops 80592896 | bytes 1040384 | tf_op jit(solution)/shard_map/while/body/eval_jaxpr/ncrw,niw->ncri/dot_general | solution.py:70
  111.7 3.6 %fusion.198 = f32[64,2,128]{2,1,0:T(2,128)S(1)} fusion(bf16[64,2,12,144]{3,2,1,0:T(8,128)(2,1)S(1)} %constant_dynamic-update-slice_fusion.383, f32[64,128]{1,0:T(8,128)S(1)} %add_multiply_fusion.12, s32[64,128]{1,0:T(8,128)S(1)} %add_select_fusion.4, s32[128,144]{0,1:T(8,128)S(1)} %iota_subtract_fusion.5, f32[64,12,128]{2,1,0:T(8,128)S(1)} %fusion.197), kind=kOutput, calls=%fused_computation.235.clone.1 | convolution fusion | flops 80592896 | bytes 1040384 | tf_op jit(solution)/shard_map/while/body/eval_jaxpr/ncrw,niw->ncri/dot_general | solution.py:70
  120.4 3.6 %fusion.205 = f32[64,2,128]{2,1,0:T(2,128)S(1)} fusion(bf16[64,2,12,144]{3,2,1,0:T(8,128)(2,1)S(1)} %constant_dynamic-update-slice_fusion.383, f32[64,128]{1,0:T(8,128)S(1)} %add_multiply_fusion.16, s32[64,128]{1,0:T(8,128)S(1)} %add_select_fusion.4, s32[128,144]{0,1:T(8,128)S(1)} %iota_subtract_fusion.5, f32[64,12,128]{2,1,0:T(8,128)S(1)} %fusion.204), kind=kOutput, calls=%fused_computation.237.clone.1 | convolution fusion | flops 80592896 | bytes 1040384 | tf_op jit(solution)/shard_map/while/body/eval_jaxpr/ncrw,niw->ncri/dot_general | solution.py:70
  132.7 3.6 %fusion.198 = f32[64,2,128]{2,1,0:T(2,128)S(1)} fusion(bf16[64,2,12,144]{3,2,1,0:T(8,128)(2,1)S(1)} %constant_dynamic-update-slice_fusion.383, f32[64,128]{1,0:T(8,128)S(1)} %add_multiply_fusion.12, s32[64,128]{1,0:T(8,128)S(1)} %add_select_fusion.4, s32[128,144]{0,1:T(8,128)S(1)} %iota_subtract_fusion.5, f32[64,12,128]{2,1,0:T(8,128)S(1)} %fusion.197), kind=kOutput, calls=%fused_computation.235.clone.1 | convolution fusion | flops 80592896 | bytes 1040384 | tf_op jit(solution)/shard_map/while/body/eval_jaxpr/ncrw,niw->ncri/dot_general | solution.py:70
  141.5 3.6 %fusion.205 = f32[64,2,128]{2,1,0:T(2,128)S(1)} fusion(bf16[64,2,12,144]{3,2,1,0:T(8,128)(2,1)S(1)} %constant_dynamic-update-slice_fusion.383, f32[64,128]{1,0:T(8,128)S(1)} %add_multiply_fusion.16, s32[64,128]{1,0:T(8,128)S(1)} %add_select_fusion.4, s32[128,144]{0,1:T(8,128)S(1)} %iota_subtract_fusion.5, f32[64,12,128]{2,1,0:T(8,128)S(1)} %fusion.204), kind=kOutput, calls=%fused_computation.237.clone.1 | convolution fusion | flops 80592896 | bytes 1040384 | tf_op jit(solution)/shard_map/while/body/eval_jaxpr/ncrw,niw->ncri/dot_general | solution.py:70
  153.8 3.6 %fusion.198 = f32[64,2,128]{2,1,0:T(2,128)S(1)} fusion(bf16[64,2,12,144]{3,2,1,0:T(8,128)(2,1)S(1)} %constant_dynamic-update-slice_fusion.383, f32[64,128]{1,0:T(8,128)S(1)} %add_multiply_fusion.12, s32[64,128]{1,0:T(8,128)S(1)} %add_select_fusion.4, s32[128,144]{0,1:T(8,128)S(1)} %iota_subtract_fusion.5, f32[64,12,128]{2,1,0:T(8,128)S(1)} %fusion.197), kind=kOutput, calls=%fused_computation.235.clone.1 | convolution fusion | flops 80592896 | bytes 1040384 | tf_op jit(solution)/shard_map/while/body/eval_jaxpr/ncrw,niw->ncri/dot_general | solution.py:70
  162.6 3.6 %fusion.205 = f32[64,2,128]{2,1,0:T(2,128)S(1)} fusion(bf16[64,2,12,144]{3,2,1,0:T(8,128)(2,1)S(1)} %constant_dynamic-update-slice_fusion.383, f32[64,128]{1,0:T(8,128)S(1)} %add_multiply_fusion.16, s32[64,128]{1,0:T(8,128)S(1)} %add_select_fusion.4, s32[128,144]{0,1:T(8,128)S(1)} %iota_subtract_fusion.5, f32[64,12,128]{2,1,0:T(8,128)S(1)} %fusion.204), kind=kOutput, calls=%fused_computation.237.clone.1 | convolution fusion | flops 80592896 | bytes 1040384 | tf_op jit(solution)/shard_map/while/body/eval_jaxpr/ncrw,niw->ncri/dot_general | solution.py:70
  174.9 3.6 %fusion.198 = f32[64,2,128]{2,1,0:T(2,128)S(1)} fusion(bf16[64,2,12,144]{3,2,1,0:T(8,128)(2,1)S(1)} %constant_dynamic-update-slice_fusion.383, f32[64,128]{1,0:T(8,128)S(1)} %add_multiply_fusion.12, s32[64,128]{1,0:T(8,128)S(1)} %add_select_fusion.4, s32[128,144]{0,1:T(8,128)S(1)} %iota_subtract_fusion.5, f32[64,12,128]{2,1,0:T(8,128)S(1)} %fusion.197), kind=kOutput, calls=%fused_computation.235.clone.1 | convolution fusion | flops 80592896 | bytes 1040384 | tf_op jit(solution)/shard_map/while/body/eval_jaxpr/ncrw,niw->ncri/dot_general | solution.py:70
  183.7 3.6 %fusion.205 = f32[64,2,128]{2,1,0:T(2,128)S(1)} fusion(bf16[64,2,12,144]{3,2,1,0:T(8,128)(2,1)S(1)} %constant_dynamic-update-slice_fusion.383, f32[64,128]{1,0:T(8,128)S(1)} %add_multiply_fusion.16, s32[64,128]{1,0:T(8,128)S(1)} %add_select_fusion.4, s32[128,144]{0,1:T(8,128)S(1)} %iota_subtract_fusion.5, f32[64,12,128]{2,1,0:T(8,128)S(1)} %fusion.204), kind=kOutput, calls=%fused_computation.237.clone.1 | convolution fusion | flops 80592896 | bytes 1040384 | tf_op jit(solution)/shard_map/while/body/eval_jaxpr/ncrw,niw->ncri/dot_general | solution.py:70
  196.0 3.6 %fusion.198 = f32[64,2,128]{2,1,0:T(2,128)S(1)} fusion(bf16[64,2,12,144]{3,2,1,0:T(8,128)(2,1)S(1)} %constant_dynamic-update-slice_fusion.383, f32[64,128]{1,0:T(8,128)S(1)} %add_multiply_fusion.12, s32[64,128]{1,0:T(8,128)S(1)} %add_select_fusion.4, s32[128,144]{0,1:T(8,128)S(1)} %iota_subtract_fusion.5, f32[64,12,128]{2,1,0:T(8,128)S(1)} %fusion.197), kind=kOutput, calls=%fused_computation.235.clone.1 | convolution fusion | flops 80592896 | bytes 1040384 | tf_op jit(solution)/shard_map/while/body/eval_jaxpr/ncrw,niw->ncri/dot_general | solution.py:70
  204.8 3.6 %fusion.205 = f32[64,2,128]{2,1,0:T(2,128)S(1)} fusion(bf16[64,2,12,144]{3,2,1,0:T(8,128)(2,1)S(1)} %constant_dynamic-update-slice_fusion.383, f32[64,128]{1,0:T(8,128)S(1)} %add_multiply_fusion.16, s32[64,128]{1,0:T(8,128)S(1)} %add_select_fusion.4, s32[128,144]{0,1:T(8,128)S(1)} %iota_subtract_fusion.5, f32[64,12,128]{2,1,0:T(8,128)S(1)} %fusion.204), kind=kOutput, calls=%fused_computation.237.clone.1 | convolution fusion | flops 80592896 | bytes 1040384 | tf_op jit(solution)/shard_map/while/body/eval_jaxpr/ncrw,niw->ncri/dot_general | solution.py:70
  212.3 146.3 %while.29 = (s32[]{:T(128)}, bf16[8,7,16,512]{3,2,0,1:T(8,128)(2,1)}, s32[8]{0:T(128)S(1)}, bf16[7,8,36,528]{3,2,0,1:T(8,128)(2,1)}, s32[2,8,16,512]{3,2,1,0:T(8...) while((s32[]{:T(128)}, ...), condition=%wide.region_7.8_spmd, body=%wide.region_5.7_spmd.sunk | while | flops 359262368 | bytes 27186292 | solution.py:165
  222.5 7.2 %multiply_reduce_fusion.2 = bf16[64,7,128]{2,1,0:T(8,128)(2,1)S(1)} fusion(f32[64,20,128]{2,1,0:T(8,128)S(1)} %fusion.190, bf16[64,7,20,144]{3,2,1,0:T(8,128)(2,1)} %copy-done.1, f32[64,128]{1,0:T(8,128)S(1)} %bitcast.958, s32[64,128]{1,0:T(8,128)S(1)} %sub.1205, s32[128,144]{0,1:T(8,128)S(1)} %iota_subtract_fusion.4), kind=kOutput, calls=%fused_computation.2.clone.1 | convolution fusion | flops 356130816 | bytes 3489792 | tf_op jit(solution)/shard_map/while/body/eval_jaxpr/ncrw,niw->ncri/dot_general | solution.py:70
  240.8 7.2 %multiply_reduce_fusion.2 = bf16[64,7,128]{2,1,0:T(8,128)(2,1)S(1)} fusion(f32[64,20,128]{2,1,0:T(8,128)S(1)} %fusion.190, bf16[64,7,20,144]{3,2,1,0:T(8,128)(2,1)} %copy-done.1, f32[64,128]{1,0:T(8,128)S(1)} %bitcast.958, s32[64,128]{1,0:T(8,128)S(1)} %sub.1205, s32[128,144]{0,1:T(8,128)S(1)} %iota_subtract_fusion.4), kind=kOutput, calls=%fused_computation.2.clone.1 | convolution fusion | flops 356130816 | bytes 3489792 | tf_op jit(solution)/shard_map/while/body/eval_jaxpr/ncrw,niw->ncri/dot_general | solution.py:70
  259.1 7.2 %multiply_reduce_fusion.2 = bf16[64,7,128]{2,1,0:T(8,128)(2,1)S(1)} fusion(f32[64,20,128]{2,1,0:T(8,128)S(1)} %fusion.190, bf16[64,7,20,144]{3,2,1,0:T(8,128)(2,1)} %copy-done.1, f32[64,128]{1,0:T(8,128)S(1)} %bitcast.958, s32[64,128]{1,0:T(8,128)S(1)} %sub.1205, s32[128,144]{0,1:T(8,128)S(1)} %iota_subtract_fusion.4), kind=kOutput, calls=%fused_computation.2.clone.1 | convolution fusion | flops 356130816 | bytes 3489792 | tf_op jit(solution)/shard_map/while/body/eval_jaxpr/ncrw,niw->ncri/dot_general | solution.py:70
  277.4 7.2 %multiply_reduce_fusion.2 = bf16[64,7,128]{2,1,0:T(8,128)(2,1)S(1)} fusion(f32[64,20,128]{2,1,0:T(8,128)S(1)} %fusion.190, bf16[64,7,20,144]{3,2,1,0:T(8,128)(2,1)} %copy-done.1, f32[64,128]{1,0:T(8,128)S(1)} %bitcast.958, s32[64,128]{1,0:T(8,128)S(1)} %sub.1205, s32[128,144]{0,1:T(8,128)S(1)} %iota_subtract_fusion.4), kind=kOutput, calls=%fused_computation.2.clone.1 | convolution fusion | flops 356130816 | bytes 3489792 | tf_op jit(solution)/shard_map/while/body/eval_jaxpr/ncrw,niw->ncri/dot_general | solution.py:70
  295.7 7.2 %multiply_reduce_fusion.2 = bf16[64,7,128]{2,1,0:T(8,128)(2,1)S(1)} fusion(f32[64,20,128]{2,1,0:T(8,128)S(1)} %fusion.190, bf16[64,7,20,144]{3,2,1,0:T(8,128)(2,1)} %copy-done.1, f32[64,128]{1,0:T(8,128)S(1)} %bitcast.958, s32[64,128]{1,0:T(8,128)S(1)} %sub.1205, s32[128,144]{0,1:T(8,128)S(1)} %iota_subtract_fusion.4), kind=kOutput, calls=%fused_computation.2.clone.1 | convolution fusion | flops 356130816 | bytes 3489792 | tf_op jit(solution)/shard_map/while/body/eval_jaxpr/ncrw,niw->ncri/dot_general | solution.py:70
  313.9 7.2 %multiply_reduce_fusion.2 = bf16[64,7,128]{2,1,0:T(8,128)(2,1)S(1)} fusion(f32[64,20,128]{2,1,0:T(8,128)S(1)} %fusion.190, bf16[64,7,20,144]{3,2,1,0:T(8,128)(2,1)} %copy-done.1, f32[64,128]{1,0:T(8,128)S(1)} %bitcast.958, s32[64,128]{1,0:T(8,128)S(1)} %sub.1205, s32[128,144]{0,1:T(8,128)S(1)} %iota_subtract_fusion.4), kind=kOutput, calls=%fused_computation.2.clone.1 | convolution fusion | flops 356130816 | bytes 3489792 | tf_op jit(solution)/shard_map/while/body/eval_jaxpr/ncrw,niw->ncri/dot_general | solution.py:70
  332.2 7.2 %multiply_reduce_fusion.2 = bf16[64,7,128]{2,1,0:T(8,128)(2,1)S(1)} fusion(f32[64,20,128]{2,1,0:T(8,128)S(1)} %fusion.190, bf16[64,7,20,144]{3,2,1,0:T(8,128)(2,1)} %copy-done.1, f32[64,128]{1,0:T(8,128)S(1)} %bitcast.958, s32[64,128]{1,0:T(8,128)S(1)} %sub.1205, s32[128,144]{0,1:T(8,128)S(1)} %iota_subtract_fusion.4), kind=kOutput, calls=%fused_computation.2.clone.1 | convolution fusion | flops 356130816 | bytes 3489792 | tf_op jit(solution)/shard_map/while/body/eval_jaxpr/ncrw,niw->ncri/dot_general | solution.py:70
  350.5 7.2 %multiply_reduce_fusion.2 = bf16[64,7,128]{2,1,0:T(8,128)(2,1)S(1)} fusion(f32[64,20,128]{2,1,0:T(8,128)S(1)} %fusion.190, bf16[64,7,20,144]{3,2,1,0:T(8,128)(2,1)} %copy-done.1, f32[64,128]{1,0:T(8,128)S(1)} %bitcast.958, s32[64,128]{1,0:T(8,128)S(1)} %sub.1205, s32[128,144]{0,1:T(8,128)S(1)} %iota_subtract_fusion.4), kind=kOutput, calls=%fused_computation.2.clone.1 | convolution fusion | flops 356130816 | bytes 3489792 | tf_op jit(solution)/shard_map/while/body/eval_jaxpr/ncrw,niw->ncri/dot_general | solution.py:70
  (1476 shorter events, 173.4 us)
Async XLA Ops:
  0.0 21.8 %copy-start = (bf16[7,8,16,512]{3,2,1,0:T(8,128)(2,1)S(1)}, bf16[7,8,16,512]{3,2,1,0:T(8,128)(2,1)}, u32[]{:S(2)}) copy-start(bf16[7,8,16,512]{3,2,1,0:T(8,128)(2,1)} %param.7) | copy-start | bytes 2752516
  1.9 26.5 %copy-start.2 = (s32[2,1,1]{0,2,1:T(1,128)S(1)}, s32[2,1,1]{0,2,1:T(1,128)}, u32[]{:S(2)}) copy-start(s32[2,1,1]{0,2,1:T(1,128)} %param.8) | copy-start | bytes 28
  2.3 16.5 %collective-permute-start = (bf16[7,8,10,512]{3,1,2,0:T(8,128)(2,1)S(1)}, bf16[7,8,10,512]{3,1,2,0:T(8,128)(2,1)S(1)}, u32[]{:S(2)}, u32[]{:S(2)}) collective-permute-start(bf16[7,8,10,512]{3,1,2,0:T(8,128)(2,1)S(1)} %copy.79), channel_id=1, source_target_pairs={{0,1},{1,2},{2,3},{3,4},{4,5},{5,6},{6,7},{7,8},{8,9},{9,10},{10,1... | collective-permute-start | bytes 1720328 | tf_op jit(solution)/shard_map/ppermute | solution.py:19
  6.4 15.2 %collective-permute-start.1 = (bf16[7,8,10,512]{3,1,2,0:T(8,128)(2,1)S(1)}, bf16[7,8,10,512]{3,1,2,0:T(8,128)(2,1)S(1)}, u32[]{:S(2)}, u32[]{:S(2)}) collective-permute-start(bf16[7,8,10,512]{3,1,2,0:T(8,128)(2,1)S(1)} %copy.80), channel_id=1, source_target_pairs={{1,0},{2,1},{3,2},{4,3},{5,4},{6,5},{7,6},{8,7},{9,8},{10,9},{11,1... | collective-permute-start | bytes 1720328 | tf_op jit(solution)/shard_map/ppermute | solution.py:19
  24.6 5.7 %collective-permute-start.2 = (bf16[8,2016]{1,0:T(8,128)(2,1)S(1)}, bf16[8,2016]{1,0:T(8,128)(2,1)S(1)}, u32[]{:S(2)}, u32[]{:S(2)}) collective-permute-start(bf16[8,2016]{1,0:T(8,128)(2,1)S(1)} %reshape.788), channel_id=1, source_target_pairs={{0,32},{32,64},{64,96},{96,128},{128,160},{160,192},{192,224},{224... | collective-permute-start | bytes 96776 | tf_op jit(solution)/shard_map/ppermute | solution.py:25
  28.1 6.7 %collective-permute-start.3 = (bf16[8,2016]{1,0:T(8,128)(2,1)S(1)}, bf16[8,2016]{1,0:T(8,128)(2,1)}, u32[]{:S(2)}, u32[]{:S(2)}) collective-permute-start(bf16[8,2016]{1,0:T(8,128)(2,1)S(1)} %reshape.790), channel_id=1, source_target_pairs={{0,224},{32,0},{64,32},{96,64},{128,96},{160,128},{192,160},{224,1... | collective-permute-start | bytes 96776 | tf_op jit(solution)/shard_map/ppermute | solution.py:25
  217.6 2.4 copy-start.1
  235.8 2.4 copy-start.1
  254.1 2.4 copy-start.1
  272.4 2.4 copy-start.1
  290.7 2.4 copy-start.1
  309.0 2.4 copy-start.1
  327.3 2.4 copy-start.1
  345.5 2.4 copy-start.1
where the time goes:
time: 362 us; the launch traced here: 359 us
  matrix products  145 us (40%)
  local copies, waits for them, and re-layouts  122 us (34%)
  loops' own time  37.2 us (10%)
  other arithmetic  27.8 us (8%)
  waiting for transfers between devices  16.9 us (5%)
  starting transfers between devices  8.86 us (2%)
    dot_general x32, matrix products, band_sample(): jnp.einsum('ncrw,niw->ncri', windows, band_weight, preferred_element_type...  145 us
    while x1040, local copies, waits for them, and re-layouts  36.1 us
    dynamic_update_slice x16, local copies, waits for them, and re-layouts, on_device(): lax.map(track_level, jnp.arange(levels, dtype=jnp.int32))  28.3 us
    another operation x1, loops' own time, on_device(): lax.map(track_level, jnp.arange(levels, dtype=jnp.int32))  19.1 us
    another operation x1, loops' own time, on_device(): advected = lax.map(advect_level, jnp.arange(levels, dtype=jnp.int32))  18.1 us
    select_n x32, other arithmetic, keys_kernel(): jnp.where(magnitude <= 1.0, near_part, jnp.where(magnitude < 2.0, far_par...  13.9 us
    ppermute x2, waiting for transfers between devices, passed_along(): return lax.ppermute(value, axis, pairs)  13 us
    dynamic_slice x16, local copies, waits for them, and re-layouts, on_device(): lax.map(track_level, jnp.arange(levels, dtype=jnp.int32))  9.21 us
  transfers between devices with their start and end apart: 4, of which 3 were waited for; matrix products, arithmetic and copies ran while one was open for 1% of the time, Pallas kernels for 0%

commit v1 on v0

v1 whole, which is shorter than its diff:
```python
import math

import jax
import jax.numpy as jnp
from jax import lax
from jax.experimental import pallas as pl
from jax.experimental.pallas import tpu as pltpu
from jax.sharding import PartitionSpec as P

HO = 8
HL = 10
ITERS = 3
WEST = 7
LANES = 128
F32 = jnp.float32
BF16 = jnp.bfloat16

courant = 2.0


def passed_along(value, axis, by):
    devices = lax.axis_size(axis)
    pairs = [(i, i + by) for i in range(devices) if 0 <= i + by < devices]
    return lax.ppermute(value, axis, pairs)


def from_behind(value, axis, steps):
    count = lax.axis_size(axis)
    pairs = [(source, (source + steps) % count) for source in range(count)]
    return lax.ppermute(value, axis, pairs)


def iota(shape, dim):
    return lax.broadcasted_iota(jnp.int32, shape, dim)


def cubic_weights(t):
    near = (1.5 * t - 2.5) * t * t + 1.0
    s = 1.0 - t
    first = -0.5 * t * s * s
    last = -0.5 * s * t * t
    third = (1.5 * s - 2.5) * s * s + 1.0
    return first, near, third, last


def edge_kernel(fields_ref, edge_west_ref, edge_east_ref, stage):
    channels, levels, rows, cols = fields_ref.shape
    stage[pl.ds(7, rows, stride=8), :] = jnp.zeros((rows, LANES), F32)
    group = iota((8, LANES), 1) // 8
    lane = iota((rows, LANES), 1)

    def pack_level(k, carry):
        for c in range(channels):
            first = pltpu.roll(fields_ref[c, k, :, :LANES].astype(F32), WEST, 1)
            last = pltpu.roll(fields_ref[c, k, :, cols - LANES :].astype(F32), WEST, 1)
            stage[pl.ds(c, rows, stride=8), :] = jnp.where(lane < WEST, last, first)
        west = jnp.zeros((8, LANES), F32)
        east = jnp.zeros((8, LANES), F32)
        for r in range(rows):
            row = stage[8 * r : 8 * r + 8, :]
            slot = rows - 1 - r
            east = jnp.where(group == slot, pltpu.roll(row, 8 * slot, 1), east)
            west = jnp.where(group == slot, pltpu.roll(row, (8 * slot - WEST) % LANES, 1), west)
        edge_west_ref[k] = west.astype(BF16)
        edge_east_ref[k] = east.astype(BF16)
        return carry

    lax.fori_loop(0, levels, pack_level, 0)


def pack_kernel(fields_ref, own_ref, down_ref, up_ref, stage):
    channels, levels, rows, cols = fields_ref.shape
    for t in range(cols // LANES):
        stage[t, pl.ds(7, rows, stride=8), :] = jnp.zeros((rows, LANES), F32)

    def pack_level(k, carry):
        for c in range(channels):
            turned = pltpu.roll(fields_ref[c, k].astype(F32), WEST, 1)
            for t in range(cols // LANES):
                stage[t, pl.ds(c, rows, stride=8), :] = turned[:, LANES * t : LANES * (t + 1)]
        for t in range(cols // LANES):
            cc = slice(LANES * t, LANES * (t + 1))
            own_ref[k, :, cc] = stage[t].astype(BF16)
            down_ref[k, :, cc] = stage[t, (rows - HL) * 8 :, :].astype(BF16)
            up_ref[k, :, cc] = stage[t, : HL * 8, :].astype(BF16)
        return carry

    lax.fori_loop(0, levels, pack_level, 0)


def fill_band_tables(mask, lane_pos):
    offset = iota(mask.shape, 0) - (iota(mask.shape, 1) & (LANES - 1))
    mask[...] = jnp.where((offset >= 0) & (offset < 16), 1.0, 0.0).astype(BF16)
    lane_pos[...] = ((iota(lane_pos.shape, 0) - iota(lane_pos.shape, 1)) & 15).astype(F32)


def band_matrix(compact, mask):
    tiles = [compact * mask[16 * t : 16 * t + 16, :] for t in range(9)]
    tiles.append(jnp.zeros((112, 256), BF16))
    return jnp.concatenate(tiles, axis=0)


def track_kernel(
    wind_ref, above_ref, below_ref, west_ref, east_ref, cells_ref, param_ref,
    row_frac_ref, col_frac_ref,
    stage, spread, mask, lane_pos, dense, taps,
):
    _, levels, rows, cols = wind_ref.shape
    fill_band_tables(mask, lane_pos)

    def edge(west, east, c, first, count):
        def tall(packed, shift):
            parts = []
            for h in range(2):
                part = jnp.broadcast_to(packed[c : c + 1, :].astype(F32), (8, LANES))
                part = pltpu.roll(part, shift + 64 * h, 1)
                parts.append(pltpu.roll(part, 0, 1, stride=8, stride_axis=0))
            return jnp.concatenate(parts, axis=0)

        lane = iota((16, LANES), 1)
        return jnp.where(lane < WEST, tall(west, 8), tall(east, 8 + WEST))[first : first + count]

    def track_level(k, carry):
        lane = iota((32, LANES), 1)
        for c in range(2):
            above = above_ref[k, 8 * c : 8 * c + 8, :].astype(F32)
            below = below_ref[k, 8 * c : 8 * c + 8, :].astype(F32)
            own = wind_ref[c, k].astype(F32)
            turned = pltpu.roll(jnp.concatenate([above, own, below], axis=0), WEST, 1)
            halo = jnp.concatenate(
                [
                    edge(above_ref[k, 16:24, :LANES], above_ref[k, 16:24, LANES : 2 * LANES], c, 8, 8),
                    edge(west_ref[k], east_ref[k], c, 0, 16),
                    edge(below_ref[k, 16:24, :LANES], below_ref[k, 16:24, LANES : 2 * LANES], c, 0, 8),
                ],
                axis=0,
            )
            first = turned[:, :LANES]
            extended = jnp.concatenate(
                [
                    jnp.where(lane < WEST, halo, first),
                    turned[:, LANES:],
                    jnp.where(lane < WEST, first, jnp.where(lane < 15, halo, 0.0)),
                ],
                axis=1,
            )
            for b in range(4):
                moved = extended if b == 0 else pltpu.roll(extended, cols + LANES - b, 1)
                for t in range(cols // LANES + 1):
                    stage[t, pl.ds(2 * b + c, 32, stride=8), :] = moved[:, LANES * t : LANES * (t + 1)]
        for t in range(cols // LANES + 1):
            spread[:, LANES * t : LANES * (t + 1)] = stage[t].astype(BF16)

        row_off = cells_ref[0, k]
        col_off = cells_ref[1, k]
        row_mid = row_off >> 1
        col_mid = col_off >> 1
        for t in range(cols // LANES):
            dense[t, 0:16, :] = (col_mid[:, LANES * t : LANES * (t + 1)] + 6).astype(F32)
            dense[t, 16:32, :] = (row_mid[:, LANES * t : LANES * (t + 1)] + 4).astype(F32)

        def gather(pair, carry):
            y = 2 * pair
            start = pl.multiple_of(16 * pair + 16, 16)
            for block in range(cols // LANES):
                lo = block * LANES
                halves = []
                for n in range(2):
                    at = dense[block, pl.ds(y + n, 8, stride=0), :]
                    at = jnp.concatenate([at, at], axis=0)
                    halves.append(jnp.where(lane_pos[...] == at, 1.0, 0.0))
                compact = jnp.concatenate(halves, axis=1).astype(BF16)
                found = jnp.dot(
                    spread[pl.ds(start, 112), lo : lo + 256],
                    band_matrix(compact, mask),
                    preferred_element_type=F32,
                )
                for n in range(2):
                    depth = dense[block, pl.ds(16 + y + n, 8, stride=0), :]
                    v = [
                        found[8 * (1 + n + i) : 8 * (2 + n + i), n * LANES : (n + 1) * LANES]
                        for i in range(12)
                    ]
                    whole = depth >= 8.0
                    v = [jnp.where(whole, v[i + 8], v[i]) for i in range(4)] + v[4:]
                    depth = jnp.where(whole, depth - 8.0, depth)
                    for step, count in ((4, 7), (2, 5), (1, 4)):
                        far = depth >= float(step)
                        v = [jnp.where(far, v[i + step], v[i]) for i in range(count)]
                        depth = jnp.where(far, depth - float(step), depth)
                    for a in range(4):
                        taps[block, pl.ds(a * 136 + y + n, 8, stride=17), :] = v[a]
            return carry

        lax.fori_loop(0, rows // 2, gather, 0, unroll=True)

        for half in range(rows // 8):
            for tile in range(cols // LANES):
                rr = slice(8 * half, 8 * half + 8)
                cc = slice(LANES * tile, LANES * tile + LANES)
                cy = param_ref[16:24, :]
                dy = param_ref[24:32, :]
                dx = param_ref[32:40, :]
                cx = param_ref[rr, :]
                oy = row_off[rr, cc]
                ox = col_off[rr, cc]
                y_odd = (oy & 1).astype(F32)
                x_odd = (ox & 1).astype(F32)
                oyf = oy.astype(F32) + 0.5
                oxf = ox.astype(F32) + 0.5
                fy = jnp.full((8, LANES), 0.5, F32)
                fx = fy
                for _ in range(ITERS):
                    wy = cubic_weights((y_odd + fy) * 0.5)
                    wx = [w.astype(BF16).astype(F32) for w in cubic_weights((x_odd + fx) * 0.5)]
                    mid = []
                    for c in range(2):
                        total = None
                        for a in range(4):
                            along = None
                            for b in range(4):
                                base = a * 136 + (2 * b + c) * 17 + 8 * half
                                term = wx[b] * taps[tile, base : base + 8, :]
                                along = term if along is None else along + term
                            along = wy[a] * along
                            total = along if total is None else total + along
                        mid.append(total)
                    lx = dx * jnp.tanh(mid[0] * cx)
                    ly = dy * jnp.tanh(mid[1] * cy)
                    fy = 0.5 + 0.5 * jnp.tanh(0.5 * (ly - oyf))
                    fx = 0.5 + 0.5 * jnp.tanh(0.5 * (lx - oxf))
                row_frac_ref[k, rr, cc] = fy
                col_frac_ref[k, rr, cc] = fx
        return carry

    lax.fori_loop(0, levels, track_level, 0)


def advect_kernel(
    own_ref, above_ref, below_ref, west_ref, east_ref, far_above_ref, far_below_ref, cells_ref,
    row_frac_ref, col_frac_ref,
    out_ref,
    spread, mask, lane_pos, dense, result,
):
    channels, levels, rows, cols = out_ref.shape
    fill_band_tables(mask, lane_pos)

    def place(block, west, east, first, count, at):
        west = west.astype(F32)
        east = east.astype(F32)
        halo = []
        lane = iota((8, LANES), 1)
        for r in range(first, first + count):
            a = pltpu.roll(west, (8 * r + 8) % LANES, 1)
            b = pltpu.roll(east, (8 * r + 8 + WEST) % LANES, 1)
            halo.append(jnp.where(lane < WEST, a, jnp.where(lane < 15, b, 0.0)))
        halo = jnp.concatenate(halo, axis=0)
        lanes = iota((8 * count, LANES), 1)
        start = block[:, :LANES].astype(F32)
        spread[at : at + 8 * count, :LANES] = jnp.where(lanes < WEST, halo, start).astype(BF16)
        spread[at : at + 8 * count, LANES:cols] = block[:, LANES:]
        spread[at : at + 8 * count, cols:] = jnp.where(lanes < WEST, start, halo).astype(BF16)

    def advect_level(k, carry):
        place(above_ref[k], far_above_ref[k, 16:24, :LANES], far_above_ref[k, 16:24, LANES : 2 * LANES], rows - HL, HL, 0)
        place(own_ref[k], west_ref[k], east_ref[k], 0, rows, 8 * HL)
        place(below_ref[k], far_below_ref[k, 16:24, :LANES], far_below_ref[k, 16:24, LANES : 2 * LANES], 0, HL, 8 * (HL + rows))

        for t in range(cols // LANES):
            cc = slice(LANES * t, LANES * (t + 1))
            dense[t, 0:16, :] = (cells_ref[1, k, :, cc] + 6).astype(F32)
            dense[t, 16:32, :] = (cells_ref[0, k, :, cc] + 8).astype(F32)
            for i, w in enumerate(cubic_weights(col_frac_ref[k, :, cc])):
                dense[t, 32 + 16 * i : 48 + 16 * i, :] = w.astype(BF16).astype(F32)
            for i, w in enumerate(cubic_weights(row_frac_ref[k, :, cc])):
                dense[t, 96 + 16 * i : 112 + 16 * i, :] = w

        def sample(pair, carry):
            y = 2 * pair
            start = pl.multiple_of(16 * pair, 16)
            for block in range(cols // LANES):
                lo = block * LANES
                halves = []
                for n in range(2):
                    def wide(part):
                        return dense[block, pl.ds(16 * part + y + n, 8, stride=0), :]

                    at = wide(0)
                    w = [wide(2 + b) for b in range(4)]
                    both = []
                    for h in range(2):
                        rel = lane_pos[8 * h : 8 * h + 8, :] - at
                        picked = jnp.where(rel == 3.0, w[3], 0.0)
                        picked = jnp.where(rel == 2.0, w[2], picked)
                        picked = jnp.where(rel == 1.0, w[1], picked)
                        both.append(jnp.where(rel == 0.0, w[0], picked))
                    halves.append(jnp.concatenate(both, axis=0))
                compact = jnp.concatenate(halves, axis=1).astype(BF16)
                mixed = jnp.dot(
                    spread[pl.ds(start, 176), lo : lo + 256],
                    band_matrix(compact, mask),
                    preferred_element_type=F32,
                )
                for n in range(2):
                    depth = dense[block, pl.ds(16 + y + n, 8, stride=0), :]
                    v = [
                        mixed[8 * (1 + n + i) : 8 * (2 + n + i), n * LANES : (n + 1) * LANES]
                        for i in range(20)
                    ]
                    whole = depth >= 16.0
                    v = [jnp.where(whole, v[i + 16], v[i]) for i in range(4)] + v[4:]
                    depth = jnp.where(whole, depth - 16.0, depth)
                    for step, count in ((8, 11), (4, 7), (2, 5), (1, 4)):
                        far = depth >= float(step)
                        v = [jnp.where(far, v[i + step], v[i]) for i in range(count)]
                        depth = jnp.where(far, depth - float(step), depth)
                    total = None
                    for a in range(4):
                        weight = dense[block, pl.ds(96 + 16 * a + y + n, 8, stride=0), :]
                        total = weight * v[a] if total is None else total + weight * v[a]
                    result[block, pl.ds(y + n, 8, stride=17), :] = total
            return carry

        lax.fori_loop(0, rows // 2, sample, 0, unroll=True)
        for c in range(channels):
            for t in range(cols // LANES):
                cc = slice(LANES * t, LANES * (t + 1))
                out_ref[c, k, :, cc] = result[t, 17 * c : 17 * c + 16, :].astype(BF16)
        return carry

    lax.fori_loop(0, levels, advect_level, 0)


def call(kernel, outs, scratch, args, name, flops):
    moved = sum(a.size * a.dtype.itemsize for a in list(args) + list(outs))
    in_vmem = pl.BlockSpec(memory_space=pltpu.VMEM)
    return pl.pallas_call(
        kernel,
        in_specs=[in_vmem] * len(args),
        out_specs=[in_vmem] * len(outs),
        out_shape=outs,
        scratch_shapes=scratch,
        cost_estimate=pl.CostEstimate(flops=flops, bytes_accessed=moved, transcendentals=0),
        compiler_params=pltpu.CompilerParams(vmem_limit_bytes=24 << 20),
        name=name,
    )(*args)


def on_device(prognostic, halo_depth, cell_offsets):
    channels, levels, rows, cols = prognostic.shape
    tiles = cols // LANES
    shape = jax.ShapeDtypeStruct
    edge = shape((levels, 8, LANES), BF16)
    edge_west, edge_east = call(
        edge_kernel, [edge, edge], [pltpu.VMEM((8 * rows, LANES), F32)], [prognostic], "edge", 10**6
    )
    west = from_behind(edge_east, "lon", 1)
    east = from_behind(edge_west, "lon", -1)
    own, down, up = call(
        pack_kernel,
        [shape((levels, 8 * n, cols), BF16) for n in (rows, HL, HL)],
        [pltpu.VMEM((tiles, 8 * rows, LANES), F32)],
        [prognostic], "pack", 10**6,
    )

    lat_total = rows * lax.axis_size("lat")
    lat_index = (lax.axis_index("lat") * rows + jnp.arange(rows, dtype=jnp.int32)).astype(F32)
    coslat = jnp.cos((lat_index + 0.5) * (math.pi / lat_total) - 0.5 * math.pi)
    reach = halo_depth[:, 0, 0].astype(F32) - 1.0
    params = jnp.concatenate(
        [-courant / (coslat * reach[1]), jnp.repeat(jnp.stack([-courant / reach[0], reach[0], reach[1]]), 8)]
    )
    params = jnp.broadcast_to(params[:, None], (rows + 24, LANES))

    edges = jnp.concatenate([west, east, jnp.zeros((levels, 8, cols - 2 * LANES), BF16)], axis=2)
    send_down = jnp.concatenate([prognostic[0, :, rows - 8 :], prognostic[1, :, rows - 8 :], edges], axis=1)
    send_up = jnp.concatenate([prognostic[0, :, :8], prognostic[1, :, :8], edges], axis=1)
    send_down, send_up, params = lax.optimization_barrier((send_down, send_up, params))
    far_above = passed_along(send_down, "lat", 1)
    far_below = passed_along(send_up, "lat", -1)
    far_above, far_below, down, up = lax.optimization_barrier((far_above, far_below, down, up))
    above = passed_along(down, "lat", 1)
    below = passed_along(up, "lat", -1)

    frac = shape((levels, rows, cols), F32)
    row_frac, col_frac = call(
        track_kernel,
        [frac, frac],
        [
            pltpu.VMEM((tiles + 1, 8 * 32, LANES), F32),
            pltpu.VMEM((8 * 32, cols + LANES), BF16),
            pltpu.VMEM((144, 256), BF16),
            pltpu.VMEM((16, LANES), F32),
            pltpu.VMEM((tiles, 32, LANES), F32),
            pltpu.VMEM((tiles, 4 * 136, LANES), F32),
        ],
        [prognostic, far_above, far_below, west, east, cell_offsets, params],
        "track", 40 * 10**6,
    )
    return call(
        advect_kernel,
        [shape(prognostic.shape, BF16)],
        [
            pltpu.VMEM((8 * (rows + 2 * HL), cols + LANES), BF16),
            pltpu.VMEM((144, 256), BF16),
            pltpu.VMEM((16, LANES), F32),
            pltpu.VMEM((tiles, 160, LANES), F32),
            pltpu.VMEM((tiles, 136, LANES), F32),
        ],
        [own, above, below, west, east, far_above, far_below, cell_offsets, row_frac, col_frac],
        "advect", 40 * 10**6,
    )[0]


def solution(mesh):
    in_specs = (P(None, None, "lat", "lon"), P(None, "lat", "lon"), P(None, None, "lat", "lon"))
    out_specs = P(None, None, "lat", "lon")
    return jax.shard_map(
        on_device, mesh=mesh, in_specs=in_specs, out_specs=out_specs, check_vma=False
    )
```

time: 362 us -> 55.3 us (0.15)
  matrix products: 145 us -> 0 us
  local copies, waits for them, and re-layouts: 122 us -> 2.68 us
  loops' own time: 37.2 us -> 0 us
  other arithmetic: 27.8 us -> 0.92 us
  Pallas kernels: 0 us -> 24.9 us
  waiting for transfers between devices: 16.9 us -> 12.1 us
  starting transfers between devices: 8.86 us -> 13.6 us
    dot_general x32 -> x0, matrix products: 145 us -> none  [band_sample(): jnp.einsum('ncrw,niw->ncri', windows, band_weight, preferred_element_type...]
    another operation x2 -> x0, loops' own time: 37.2 us -> none  [the longest x1 19.1 us: on_device(): lax.map(track_level, jnp.arange(levels, dtype=jnp.int32))]
    while x1040 -> x0, local copies, waits for them, and re-layouts: 36.1 us -> none
    dynamic_update_slice x24 -> x0, local copies, waits for them, and re-layouts: 33.6 us -> none  [the longest x16 28.3 us: on_device(): lax.map(track_level, jnp.arange(levels, dtype=jnp.int32))]
    pallas_call x0 -> x4, Pallas kernels: none -> 24.9 us  [call(): pl.pallas_call(kernel, in_specs=[in_vmem] * len(args), out_specs=[in_vmem...]
    dynamic_slice x24 -> x0, local copies, waits for them, and re-layouts: 17.9 us -> none  [the longest x16 9.21 us: on_device(): lax.map(track_level, jnp.arange(levels, dtype=jnp.int32))]
    slice x19 -> x1, local copies, waits for them, and re-layouts: 16.4 us -> 0.59 us  [on_device(): reach[1]]
    select_n x48 -> x0, other arithmetic: 14.3 us -> none  [the longest x32 13.9 us: keys_kernel(): jnp.where(magnitude <= 1.0, near_part, jnp.where(magnitude < 2.0, far_par...]
  transfers between devices with their start and end apart: 4 -> 6, of which waited for: 3 -> 3; matrix products, arithmetic and copies ran while one was open for 1% -> 3% of each run, Pallas kernels for 0% -> 25%
where the time goes in v1:
time: 55.3 us; the launch traced here: 55 us
  Pallas kernels  24.9 us (45%)
  starting transfers between devices  13.6 us (25%)
  waiting for transfers between devices  12.1 us (22%)
  local copies, waits for them, and re-layouts  2.68 us (5%)
  other arithmetic  0.92 us (2%)
  between operations  0.81 us (1%)
    pallas_call x4, Pallas kernels, call(): pl.pallas_call(kernel, in_specs=[in_vmem] * len(args), out_specs=[in_vmem...  24.9 us
    ppermute x4, starting transfers between devices, passed_along(): return lax.ppermute(value, axis, pairs)  10.7 us
    ppermute x4, waiting for transfers between devices, passed_along(): return lax.ppermute(value, axis, pairs)  8.89 us
    ppermute x2, waiting for transfers between devices, from_behind(): return lax.ppermute(value, axis, pairs)  3.22 us
    ppermute x2, starting transfers between devices, from_behind(): return lax.ppermute(value, axis, pairs)  2.91 us
    unnamed x8, local copies, waits for them, and re-layouts  1.84 us
  transfers between devices with their start and end apart: 6, of which 3 were waited for; matrix products, arithmetic and copies ran while one was open for 3% of the time, Pallas kernels for 25%

profile of v1, /device:TPU:135, one launch (start us, length us, event | category | flops | bytes accessed | tf_op | source)
XLA Modules:
  0.0 55.0 jit_solution(7769939875462105300)
XLA Ops:
  0.0 0.0 copy-start
  0.0 1.2 %copy-done = bf16[7,8,16,512]{3,2,1,0:T(8,128)(2,1)S(1)} copy-done((bf16[7,8,16,512]{3,2,1,0:T(8,128)(2,1)S(1)}, bf16[7,8,16,512]{3,2,1,0:T(8,128)(2,1)}, u32[]{:S(2)}) %copy-start) | copy-done | bytes 917528
  1.2 0.0 copy-start.1
  1.2 1.5 %edge.1 = (bf16[8,8,128]{2,1,0:T(8,128)(2,1)S(1)}, bf16[8,8,128]{2,1,0:T(8,128)(2,1)S(1)}) custom-call(bf16[7,8,16,512]{3,2,1,0:T(8,128)(2,1)S(1)} %copy-done), custom_call_target="tpu_custom_call" | custom-call | flops 1000000 | bytes 950272 | tf_op jit(solution)/shard_map/edge/pallas_call | solution.py:337
  2.7 2.9 %collective-permute-start = (bf16[8,8,128]{2,1,0:T(8,128)(2,1)S(1)}, bf16[8,8,128]{2,1,0:T(8,128)(2,1)S(1)}, u32[]{:S(2)}, u32[]{:S(2)}) collective-permute-start(bf16[8,8,128]{2,1,0:T(8,128)(2,1)S(1)} %get-tuple-element.20), channel_id=1, source_target_pairs={{0,32},{32,64},{64,96},{96,128},{128,160},{160,192},{192,224},{224... | collective-permute-start | bytes 49160 | tf_op jit(solution)/shard_map/ppermute | solution.py:30
  5.6 0.0 collective-permute-start.1
  5.6 0.0 copy-start.3
  5.6 0.6 %copy-done.3 = s32[2,1,1]{0,2,1:T(1,128)S(1)} copy-done((s32[2,1,1]{0,2,1:T(1,128)S(1)}, s32[2,1,1]{0,2,1:T(1,128)}, u32[]{:S(2)}) %copy-start.3) | copy-done | bytes 32
  6.3 0.6 %fusion.1 = (f32[1,1,1]{0,2,1:T(1,128)}, f32[1,1,1]{0,2,1:T(1,128)}) fusion(f32[2,1,1]{0,2,1:T(1,128)S(1)} %get-tuple-element.41), kind=kLoop, calls=%fused_computation.12 | loop fusion | bytes 16 | tf_op jit(solution)/shard_map/slice | solution.py:371
  7.5 0.1 pad_maximum_fusion
  7.6 0.1 broadcast_in_dim.13
  7.7 0.1 reshape.15
  7.8 0.7 %multiply_divide_fusion = f32[16]{0:T(128)S(1)} fusion(f32[]{:T(128)} %bitcast.4, s32[]{:T(128)S(6)} %mul.12), kind=kLoop, calls=%fused_computation.9 | loop fusion | flops 112 | bytes 72 | tf_op jit(solution)/shard_map/div | solution.py:371
  8.5 0.1 pad_maximum_fusion.1
  8.6 0.0 collective-permute-done.west_ref
  8.6 3.2 %collective-permute-done.1.east_ref = bf16[8,8,128]{2,1,0:T(8,128)(2,1)S(1)} collective-permute-done((bf16[8,8,128]{2,1,0:T(8,128)(2,1)S(1)}, bf16[8,8,128]{2,1,0:T(8,128)(2,1)S(1)}, u32[]{:S(2)}, u32[]{:S(2)}) %collective-permute-start.1) | collective-permute-done | bytes 16416 | tf_op jit(solution)/shard_map/ppermute | solution.py:30
  11.8 0.1 maximum_maximum_fusion.2
  11.9 0.0 copy-start.2
  11.9 0.1 broadcast_in_dim.14.param_ref
  12.0 4.4 %collective-permute-start.2 = (bf16[8,24,512]{2,1,0:T(8,128)(2,1)S(1)}, bf16[8,24,512]{2,1,0:T(8,128)(2,1)S(1)}, u32[]{:S(2)}, u32[]{:S(2)}) collective-permute-start(bf16[8,24,512]{2,1,0:T(8,128)(2,1)S(1)} %get-tuple-element.22), channel_id=1, source_target_pairs={{0,1},{1,2},{2,3},{3,4},{4,5},{5,6},{6,7},{7,8},{8,9},{9,10},{10,1... | collective-permute-start | bytes 589832 | tf_op jit(solution)/shard_map/ppermute | solution.py:24
  16.4 1.9 %collective-permute-start.3 = (bf16[8,24,512]{2,1,0:T(8,128)(2,1)S(1)}, bf16[8,24,512]{2,1,0:T(8,128)(2,1)S(1)}, u32[]{:S(2)}, u32[]{:S(2)}) collective-permute-start(bf16[8,24,512]{2,1,0:T(8,128)(2,1)S(1)} %get-tuple-element.23), channel_id=1, source_target_pairs={{1,0},{2,1},{3,2},{4,3},{5,4},{6,5},{7,6},{8,7},{9,8},{10,9},{11,1... | collective-permute-start | bytes 589832 | tf_op jit(solution)/shard_map/ppermute | solution.py:24
  18.3 0.0 copy-done.1
  18.3 1.3 %pack.1 = (bf16[8,128,512]{2,1,0:T(8,128)(2,1)S(1)}, bf16[8,80,512]{2,1,0:T(8,128)(2,1)S(1)}, bf16[8,80,512]{2,1,0:T(8,128)(2,1)S(1)}) custom-call(bf16[7,8,16,512]{3,2,1,0:T(8,128)(2,1)S(1)} %copy-done.1), custom_call_target="tpu_custom_call" | custom-call | flops 1000000 | bytes 3276800 | tf_op jit(solution)/shard_map/pack/pallas_call | solution.py:337
  19.6 0.0 collective-permute-done.2.above_ref.far_above_ref
  19.7 5.0 %collective-permute-done.3.below_ref.far_below_ref = bf16[8,24,512]{2,1,0:T(8,128)(2,1)S(1)} collective-permute-done((bf16[8,24,512]{2,1,0:T(8,128)(2,1)S(1)}, bf16[8,24,512]{2,1,0:T(8,128)(2,1)S(1)}, u32[]{:S(2)}, u32[]{:S(2)}) %collective-permute-start.3) | collective-permute-done | bytes 196640 | tf_op jit(solution)/shard_map/ppermute | solution.py:24
  24.7 1.9 %collective-permute-start.4 = (bf16[8,80,512]{2,1,0:T(8,128)(2,1)S(1)}, bf16[8,80,512]{2,1,0:T(8,128)(2,1)S(1)}, u32[]{:S(2)}, u32[]{:S(2)}) collective-permute-start(bf16[8,80,512]{2,1,0:T(8,128)(2,1)S(1)} %get-tuple-element.26), channel_id=1, source_target_pairs={{0,1},{1,2},{2,3},{3,4},{4,5},{5,6},{6,7},{7,8},{8,9},{9,10},{10,1... | collective-permute-start | bytes 1966088 | tf_op jit(solution)/shard_map/ppermute | solution.py:24
  26.6 2.4 %collective-permute-start.5 = (bf16[8,80,512]{2,1,0:T(8,128)(2,1)S(1)}, bf16[8,80,512]{2,1,0:T(8,128)(2,1)S(1)}, u32[]{:S(2)}, u32[]{:S(2)}) collective-permute-start(bf16[8,80,512]{2,1,0:T(8,128)(2,1)S(1)} %get-tuple-element.27), channel_id=1, source_target_pairs={{1,0},{2,1},{3,2},{4,3},{5,4},{6,5},{7,6},{8,7},{9,8},{10,9},{11,1... | collective-permute-start | bytes 1966088 | tf_op jit(solution)/shard_map/ppermute | solution.py:24
  29.0 0.0 copy-done.2
  29.0 12.6 %track.1 = (f32[8,16,512]{2,1,0:T(8,128)S(1)}, f32[8,16,512]{2,1,0:T(8,128)S(1)}) custom-call(bf16[7,8,16,512]{3,2,1,0:T(8,128)(2,1)S(1)} %copy-done.1, bf16[8,24,512]{2,1,0:T(8,128)(2,1)S(1)} %collective-permute-done.2.above_ref.far_above_ref, bf16[8,24,512]{2,1,0:T(8,128)(2,1)S(1)} %collective-permute-done.3.below_ref.far_below_ref, ...), custom_call_target="tpu_custom_call" | custom-call | flops 40000000 | bytes 2412544 | tf_op jit(solution)/shard_map/track/pallas_call | solution.py:337
  41.7 0.0 collective-permute-done.4.above_ref
  41.7 3.8 %collective-permute-done.5.below_ref = bf16[8,80,512]{2,1,0:T(8,128)(2,1)S(1)} collective-permute-done((bf16[8,80,512]{2,1,0:T(8,128)(2,1)S(1)}, bf16[8,80,512]{2,1,0:T(8,128)(2,1)S(1)}, u32[]{:S(2)}, u32[]{:S(2)}) %collective-permute-start.5) | collective-permute-done | bytes 655392 | tf_op jit(solution)/shard_map/ppermute | solution.py:24
  45.5 9.5 %advect.1 = bf16[7,8,16,512]{3,2,1,0:T(8,128)(2,1)} custom-call(bf16[8,128,512]{2,1,0:T(8,128)(2,1)S(1)} %get-tuple-element.19.own_ref, bf16[8,80,512]{2,1,0:T(8,128)(2,1)S(1)} %collective-permute-done.4.above_ref, bf16[8,80,512]{2,1,0:T(8,128)(2,1)S(1)} %collective-permute-done.5.below_ref, bf16[8,8,128]{2,1,0:T(8,128)(2,1)S(1)} %collective-permute-done.west_ref, ...), custom_call_target="tpu_custom_call" | custom-call | flops 40000000 | bytes 4751360 | tf_op jit(solution)/shard_map/advect/pallas_call | solution.py:337
  (4 shorter events, 0.0 us)
Async XLA Ops:
  0.0 1.2 %copy-start = (bf16[7,8,16,512]{3,2,1,0:T(8,128)(2,1)S(1)}, bf16[7,8,16,512]{3,2,1,0:T(8,128)(2,1)}, u32[]{:S(2)}) copy-start(bf16[7,8,16,512]{3,2,1,0:T(8,128)(2,1)} %wind_ref.1) | copy-start | bytes 2752516
  1.2 17.1 %copy-start.1 = (bf16[7,8,16,512]{3,2,1,0:T(8,128)(2,1)S(1)}, bf16[7,8,16,512]{3,2,1,0:T(8,128)(2,1)}, u32[]{:S(2)}) copy-start(bf16[7,8,16,512]{3,2,1,0:T(8,128)(2,1)} %wind_ref.1) | copy-start | bytes 2752516
  2.7 5.9 %collective-permute-start = (bf16[8,8,128]{2,1,0:T(8,128)(2,1)S(1)}, bf16[8,8,128]{2,1,0:T(8,128)(2,1)S(1)}, u32[]{:S(2)}, u32[]{:S(2)}) collective-permute-start(bf16[8,8,128]{2,1,0:T(8,128)(2,1)S(1)} %get-tuple-element.20), channel_id=1, source_target_pairs={{0,32},{32,64},{64,96},{96,128},{128,160},{160,192},{192,224},{224... | collective-permute-start | bytes 49160 | tf_op jit(solution)/shard_map/ppermute | solution.py:30
  5.6 6.2 %collective-permute-start.1 = (bf16[8,8,128]{2,1,0:T(8,128)(2,1)S(1)}, bf16[8,8,128]{2,1,0:T(8,128)(2,1)S(1)}, u32[]{:S(2)}, u32[]{:S(2)}) collective-permute-start(bf16[8,8,128]{2,1,0:T(8,128)(2,1)S(1)} %get-tuple-element.21), channel_id=1, source_target_pairs={{0,224},{32,0},{64,32},{96,64},{128,96},{160,128},{192,160},{224,1... | collective-permute-start | bytes 49160 | tf_op jit(solution)/shard_map/ppermute | solution.py:30
  5.6 0.7 %copy-start.3 = (s32[2,1,1]{0,2,1:T(1,128)S(1)}, s32[2,1,1]{0,2,1:T(1,128)}, u32[]{:S(2)}) copy-start(s32[2,1,1]{0,2,1:T(1,128)} %param.4) | copy-start | bytes 28
  11.9 17.2 %copy-start.2 = (s32[2,8,16,512]{3,2,1,0:T(8,128)S(1)}, s32[2,8,16,512]{3,2,1,0:T(8,128)}, u32[]{:S(2)}) copy-start(s32[2,8,16,512]{3,2,1,0:T(8,128)} %cells_ref.3) | copy-start | bytes 1572868
  12.0 7.7 %collective-permute-start.2 = (bf16[8,24,512]{2,1,0:T(8,128)(2,1)S(1)}, bf16[8,24,512]{2,1,0:T(8,128)(2,1)S(1)}, u32[]{:S(2)}, u32[]{:S(2)}) collective-permute-start(bf16[8,24,512]{2,1,0:T(8,128)(2,1)S(1)} %get-tuple-element.22), channel_id=1, source_target_pairs={{0,1},{1,2},{2,3},{3,4},{4,5},{5,6},{6,7},{7,8},{8,9},{9,10},{10,1... | collective-permute-start | bytes 589832 | tf_op jit(solution)/shard_map/ppermute | solution.py:24
  16.4 8.3 %collective-permute-start.3 = (bf16[8,24,512]{2,1,0:T(8,128)(2,1)S(1)}, bf16[8,24,512]{2,1,0:T(8,128)(2,1)S(1)}, u32[]{:S(2)}, u32[]{:S(2)}) collective-permute-start(bf16[8,24,512]{2,1,0:T(8,128)(2,1)S(1)} %get-tuple-element.23), channel_id=1, source_target_pairs={{1,0},{2,1},{3,2},{4,3},{5,4},{6,5},{7,6},{8,7},{9,8},{10,9},{11,1... | collective-permute-start | bytes 589832 | tf_op jit(solution)/shard_map/ppermute | solution.py:24
  24.7 17.0 %collective-permute-start.4 = (bf16[8,80,512]{2,1,0:T(8,128)(2,1)S(1)}, bf16[8,80,512]{2,1,0:T(8,128)(2,1)S(1)}, u32[]{:S(2)}, u32[]{:S(2)}) collective-permute-start(bf16[8,80,512]{2,1,0:T(8,128)(2,1)S(1)} %get-tuple-element.26), channel_id=1, source_target_pairs={{0,1},{1,2},{2,3},{3,4},{4,5},{5,6},{6,7},{7,8},{8,9},{9,10},{10,1... | collective-permute-start | bytes 1966088 | tf_op jit(solution)/shard_map/ppermute | solution.py:24
  26.6 18.9 %collective-permute-start.5 = (bf16[8,80,512]{2,1,0:T(8,128)(2,1)S(1)}, bf16[8,80,512]{2,1,0:T(8,128)(2,1)S(1)}, u32[]{:S(2)}, u32[]{:S(2)}) collective-permute-start(bf16[8,80,512]{2,1,0:T(8,128)(2,1)S(1)} %get-tuple-element.27), channel_id=1, source_target_pairs={{1,0},{2,1},{3,2},{4,3},{5,4},{6,5},{7,6},{8,7},{9,8},{10,9},{11,1... | collective-permute-start | bytes 1966088 | tf_op jit(solution)/shard_map/ppermute | solution.py:24

commit v2 on v1

--- a/solution.py
+++ b/solution.py
@@ -10,6 +10,8 @@
 HO = 8
 HL = 10
 ITERS = 3
+NEAR = 8
+FAR = HL - NEAR
 WEST = 7
 LANES = 128
 F32 = jnp.float32
@@ -68,24 +70,51 @@
     lax.fori_loop(0, levels, pack_level, 0)
 
 
+def to_row_major(fields_ref, k, stage):
+    channels, _, rows, cols = fields_ref.shape
+    for c in range(channels):
+        turned = pltpu.roll(fields_ref[c, k].astype(F32), WEST, 1)
+        for t in range(cols // LANES):
+            stage[t, pl.ds(c, rows, stride=8), :] = turned[:, LANES * t : LANES * (t + 1)]
+
+
+def clear_last_field(stage, rows):
+    for t in range(stage.shape[0]):
+        stage[t, pl.ds(7, rows, stride=8), :] = jnp.zeros((rows, LANES), F32)
+
+
 def pack_kernel(fields_ref, own_ref, down_ref, up_ref, stage):
-    channels, levels, rows, cols = fields_ref.shape
-    for t in range(cols // LANES):
-        stage[t, pl.ds(7, rows, stride=8), :] = jnp.zeros((rows, LANES), F32)
+    _, levels, rows, cols = fields_ref.shape
+    clear_last_field(stage, rows)
+    down, up = 8 * (rows - HL), 8 * NEAR
 
     def pack_level(k, carry):
-        for c in range(channels):
-            turned = pltpu.roll(fields_ref[c, k].astype(F32), WEST, 1)
-            for t in range(cols // LANES):
-                stage[t, pl.ds(c, rows, stride=8), :] = turned[:, LANES * t : LANES * (t + 1)]
+        to_row_major(fields_ref, k, stage)
         for t in range(cols // LANES):
             cc = slice(LANES * t, LANES * (t + 1))
             own_ref[k, :, cc] = stage[t].astype(BF16)
-            down_ref[k, :, cc] = stage[t, (rows - HL) * 8 :, :].astype(BF16)
-            up_ref[k, :, cc] = stage[t, : HL * 8, :].astype(BF16)
+            down_ref[k, :, cc] = stage[t, down : down + 8 * FAR, :].astype(BF16)
+            up_ref[k, :, cc] = stage[t, up : up + 8 * FAR, :].astype(BF16)
         return carry
 
     lax.fori_loop(0, levels, pack_level, 0)
+
+
+def relay_kernel(above_ref, below_ref, above_out, below_out, stage, other):
+    _, levels, rows, cols = above_ref.shape
+    clear_last_field(stage, rows)
+    clear_last_field(other, rows)
+
+    def relay_level(k, carry):
+        to_row_major(above_ref, k, stage)
+        to_row_major(below_ref, k, other)
+        for t in range(cols // LANES):
+            cc = slice(LANES * t, LANES * (t + 1))
+            above_out[k, :, cc] = stage[t].astype(BF16)
+            below_out[k, :, cc] = other[t].astype(BF16)
+        return carry
+
+    lax.fori_loop(0, levels, relay_level, 0)
 
 
 def fill_band_tables(mask, lane_pos):
@@ -101,7 +130,7 @@
 
 
 def track_kernel(
-    wind_ref, above_ref, below_ref, west_ref, east_ref, cells_ref, param_ref,
+    wind_ref, above_ref, below_ref, far_above_ref, far_below_ref, west_ref, east_ref, cells_ref, param_ref,
     row_frac_ref, col_frac_ref,
     stage, spread, mask, lane_pos, dense, taps,
 ):
@@ -123,15 +152,15 @@
     def track_level(k, carry):
         lane = iota((32, LANES), 1)
         for c in range(2):
-            above = above_ref[k, 8 * c : 8 * c + 8, :].astype(F32)
-            below = below_ref[k, 8 * c : 8 * c + 8, :].astype(F32)
+            above = above_ref[c, k].astype(F32)
+            below = below_ref[c, k].astype(F32)
             own = wind_ref[c, k].astype(F32)
             turned = pltpu.roll(jnp.concatenate([above, own, below], axis=0), WEST, 1)
             halo = jnp.concatenate(
                 [
-                    edge(above_ref[k, 16:24, :LANES], above_ref[k, 16:24, LANES : 2 * LANES], c, 8, 8),
+                    edge(far_above_ref[k, 16:24, :LANES], far_above_ref[k, 16:24, LANES : 2 * LANES], c, 8, 8),
                     edge(west_ref[k], east_ref[k], c, 0, 16),
-                    edge(below_ref[k, 16:24, :LANES], below_ref[k, 16:24, LANES : 2 * LANES], c, 0, 8),
+                    edge(far_below_ref[k, 16:24, :LANES], far_below_ref[k, 16:24, LANES : 2 * LANES], c, 0, 8),
                 ],
                 axis=0,
             )
@@ -262,10 +291,13 @@
         spread[at : at + 8 * count, cols:] = jnp.where(lanes < WEST, start, halo).astype(BF16)
 
     def advect_level(k, carry):
-        place(above_ref[k], far_above_ref[k, 16:24, :LANES], far_above_ref[k, 16:24, LANES : 2 * LANES], rows - HL, HL, 0)
+        a_west, a_east = far_above_ref[k, 16:24, :LANES], far_above_ref[k, 16:24, LANES : 2 * LANES]
+        b_west, b_east = far_below_ref[k, 16:24, :LANES], far_below_ref[k, 16:24, LANES : 2 * LANES]
+        place(far_above_ref[k, : 8 * FAR, :], a_west, a_east, rows - HL, FAR, 0)
+        place(above_ref[k], a_west, a_east, rows - NEAR, NEAR, 8 * FAR)
         place(own_ref[k], west_ref[k], east_ref[k], 0, rows, 8 * HL)
-        place(below_ref[k], far_below_ref[k, 16:24, :LANES], far_below_ref[k, 16:24, LANES : 2 * LANES], 0, HL, 8 * (HL + rows))
-
+        place(below_ref[k], b_west, b_east, 0, NEAR, 8 * (HL + rows))
+        place(far_below_ref[k, : 8 * FAR, :], b_west, b_east, NEAR, FAR, 8 * (HL + rows + NEAR))
         for t in range(cols // LANES):
             cc = slice(LANES * t, LANES * (t + 1))
             dense[t, 0:16, :] = (cells_ref[1, k, :, cc] + 6).astype(F32)
@@ -350,6 +382,8 @@
     channels, levels, rows, cols = prognostic.shape
     tiles = cols // LANES
     shape = jax.ShapeDtypeStruct
+    above = passed_along(prognostic[:, :, rows - NEAR :], "lat", 1)
+    below = passed_along(prognostic[:, :, :NEAR], "lat", -1)
     edge = shape((levels, 8, LANES), BF16)
     edge_west, edge_east = call(
         edge_kernel, [edge, edge], [pltpu.VMEM((8 * rows, LANES), F32)], [prognostic], "edge", 10**6
@@ -358,7 +392,7 @@
     east = from_behind(edge_west, "lon", -1)
     own, down, up = call(
         pack_kernel,
-        [shape((levels, 8 * n, cols), BF16) for n in (rows, HL, HL)],
+        [shape((levels, 8 * n, cols), BF16) for n in (rows, FAR, FAR)],
         [pltpu.VMEM((tiles, 8 * rows, LANES), F32)],
         [prognostic], "pack", 10**6,
     )
@@ -373,14 +407,19 @@
     params = jnp.broadcast_to(params[:, None], (rows + 24, LANES))
 
     edges = jnp.concatenate([west, east, jnp.zeros((levels, 8, cols - 2 * LANES), BF16)], axis=2)
-    send_down = jnp.concatenate([prognostic[0, :, rows - 8 :], prognostic[1, :, rows - 8 :], edges], axis=1)
-    send_up = jnp.concatenate([prognostic[0, :, :8], prognostic[1, :, :8], edges], axis=1)
+    send_down = jnp.concatenate([down, edges], axis=1)
+    send_up = jnp.concatenate([up, edges], axis=1)
     send_down, send_up, params = lax.optimization_barrier((send_down, send_up, params))
     far_above = passed_along(send_down, "lat", 1)
     far_below = passed_along(send_up, "lat", -1)
-    far_above, far_below, down, up = lax.optimization_barrier((far_above, far_below, down, up))
-    above = passed_along(down, "lat", 1)
-    below = passed_along(up, "lat", -1)
+    halo = shape((levels, 8 * NEAR, cols), BF16)
+    relayed_above, relayed_below = call(
+        relay_kernel, [halo, halo], [pltpu.VMEM((tiles, 8 * NEAR, LANES), F32)] * 2,
+        [above, below], "relay", 10**6,
+    )
+    relayed_above, relayed_below, far_above, far_below = lax.optimization_barrier(
+        (relayed_above, relayed_below, far_above, far_below)
+    )
 
     frac = shape((levels, rows, cols), F32)
     row_frac, col_frac = call(
@@ -394,7 +433,7 @@
             pltpu.VMEM((tiles, 32, LANES), F32),
             pltpu.VMEM((tiles, 4 * 136, LANES), F32),
         ],
-        [prognostic, far_above, far_below, west, east, cell_offsets, params],
+        [prognostic, above, below, far_above, far_below, west, east, cell_offsets, params],
         "track", 40 * 10**6,
     )
     return call(
@@ -407,7 +446,7 @@
             pltpu.VMEM((tiles, 160, LANES), F32),
             pltpu.VMEM((tiles, 136, LANES), F32),
         ],
-        [own, above, below, west, east, far_above, far_below, cell_offsets, row_frac, col_frac],
+        [own, relayed_above, relayed_below, west, east, far_above, far_below, cell_offsets, row_frac, col_frac],
         "advect", 40 * 10**6,
     )[0]
 

time: 55.3 us -> 60.4 us (1.092)
  the two profiles are of different devices: /device:TPU:135 before, /device:TPU:105 now
where the time goes in v2:
time: 60.4 us; the launch traced here: 60.1 us
  Pallas kernels  25.9 us (43%)
  starting transfers between devices  21.5 us (36%)
  waiting for transfers between devices  8.18 us (14%)
  local copies, waits for them, and re-layouts  2.81 us (5%)
  other arithmetic  0.91 us (2%)
  between operations  0.81 us (1%)
    pallas_call x5, Pallas kernels, call(): pl.pallas_call(kernel, in_specs=[in_vmem] * len(args), out_specs=[in_vmem...  25.9 us
    ppermute x4, starting transfers between devices, passed_along(): return lax.ppermute(value, axis, pairs)  17 us
    ppermute x4, waiting for transfers between devices, passed_along(): return lax.ppermute(value, axis, pairs)  6.09 us
    ppermute x2, starting transfers between devices, from_behind(): return lax.ppermute(value, axis, pairs)  4.58 us
    ppermute x2, waiting for transfers between devices, from_behind(): return lax.ppermute(value, axis, pairs)  2.09 us
    slice x1, local copies, waits for them, and re-layouts, on_device(): below = passed_along(prognostic[:, :, :NEAR], 'lat', -1)  1.32 us
  transfers between devices with their start and end apart: 6, of which 2 were waited for; matrix products, arithmetic and copies ran while one was open for 3% of the time, Pallas kernels for 6%

profile of v2, /device:TPU:105, one launch (start us, length us, event | category | flops | bytes accessed | tf_op | source)
XLA Modules:
  0.0 60.1 jit_solution(12286624644713966039)
XLA Ops:
  0.0 0.0 copy-start
  0.0 1.3 %fusion.1 = (bf16[7,8,8,512]{3,2,1,0:T(8,128)(2,1)S(1)}, bf16[7,8,8,512]{3,2,1,0:T(8,128)(2,1)S(1)}) fusion(bf16[7,8,16,512]{3,2,1,0:T(8,128)(2,1)} %wind_ref.1), kind=kLoop, calls=%fused_computation.8 | loop fusion | bytes 1835008 | tf_op jit(solution)/shard_map/slice | solution.py:386
  1.3 5.2 %collective-permute-start = (bf16[7,8,8,512]{3,2,1,0:T(8,128)(2,1)S(1)}, bf16[7,8,8,512]{3,2,1,0:T(8,128)(2,1)S(1)}, u32[]{:S(2)}, u32[]{:S(2)}) collective-permute-start(bf16[7,8,8,512]{3,2,1,0:T(8,128)(2,1)S(1)} %get-tuple-element.38), channel_id=1, source_target_pairs={{0,1},{1,2},{2,3},{3,4},{4,5},{5,6},{6,7},{7,8},{8,9},{9,10},{10,1... | collective-permute-start | bytes 1376264 | tf_op jit(solution)/shard_map/ppermute | solution.py:26
  6.5 1.9 %collective-permute-start.1 = (bf16[7,8,8,512]{3,2,1,0:T(8,128)(2,1)S(1)}, bf16[7,8,8,512]{3,2,1,0:T(8,128)(2,1)S(1)}, u32[]{:S(2)}, u32[]{:S(2)}) collective-permute-start(bf16[7,8,8,512]{3,2,1,0:T(8,128)(2,1)S(1)} %get-tuple-element.37), channel_id=1, source_target_pairs={{1,0},{2,1},{3,2},{4,3},{5,4},{6,5},{7,6},{8,7},{9,8},{10,9},{11,1... | collective-permute-start | bytes 1376264 | tf_op jit(solution)/shard_map/ppermute | solution.py:26
  8.5 0.0 copy-done
  8.5 1.5 %edge.1 = (bf16[8,8,128]{2,1,0:T(8,128)(2,1)S(1)}, bf16[8,8,128]{2,1,0:T(8,128)(2,1)S(1)}) custom-call(bf16[7,8,16,512]{3,2,1,0:T(8,128)(2,1)S(1)} %copy-done), custom_call_target="tpu_custom_call" | custom-call | flops 1000000 | bytes 950272 | tf_op jit(solution)/shard_map/edge/pallas_call | solution.py:369
  10.0 4.6 %collective-permute-start.3 = (bf16[8,8,128]{2,1,0:T(8,128)(2,1)S(1)}, bf16[8,8,128]{2,1,0:T(8,128)(2,1)S(1)}, u32[]{:S(2)}, u32[]{:S(2)}) collective-permute-start(bf16[8,8,128]{2,1,0:T(8,128)(2,1)S(1)} %get-tuple-element.26), channel_id=1, source_target_pairs={{0,224},{32,0},{64,32},{96,64},{128,96},{160,128},{192,160},{224,1... | collective-permute-start | bytes 49160 | tf_op jit(solution)/shard_map/ppermute | solution.py:32
  14.6 0.0 copy-start.2
  14.6 0.0 collective-permute-start.2
  14.6 0.7 %copy-done.2 = s32[2,1,1]{0,2,1:T(1,128)S(1)} copy-done((s32[2,1,1]{0,2,1:T(1,128)S(1)}, s32[2,1,1]{0,2,1:T(1,128)}, u32[]{:S(2)}) %copy-start.2) | copy-done | bytes 32
  15.2 0.6 fusion.2
  16.5 0.1 pad_maximum_fusion.2
  16.6 0.1 broadcast_in_dim.13
  16.6 0.1 reshape.15
  16.7 0.7 %multiply_divide_fusion = f32[16]{0:T(128)S(1)} fusion(f32[]{:T(128)} %bitcast, s32[]{:T(128)S(6)} %mul.12), kind=kLoop, calls=%fused_computation.5 | loop fusion | flops 112 | bytes 72 | tf_op jit(solution)/shard_map/div | solution.py:405
  17.4 0.1 pad_maximum_fusion.3
  17.5 1.2 %pack.1 = (bf16[8,128,512]{2,1,0:T(8,128)(2,1)S(1)}, bf16[8,16,512]{2,1,0:T(8,128)(2,1)S(1)}, bf16[8,16,512]{2,1,0:T(8,128)(2,1)S(1)}) custom-call(bf16[7,8,16,512]{3,2,1,0:T(8,128)(2,1)S(1)} %copy-done), custom_call_target="tpu_custom_call" | custom-call | flops 1000000 | bytes 2228224 | tf_op jit(solution)/shard_map/pack/pallas_call | solution.py:369
  18.7 0.0 collective-permute-done.3.east_ref
  18.7 2.1 %collective-permute-done.2.west_ref = bf16[8,8,128]{2,1,0:T(8,128)(2,1)S(1)} collective-permute-done((bf16[8,8,128]{2,1,0:T(8,128)(2,1)S(1)}, bf16[8,8,128]{2,1,0:T(8,128)(2,1)S(1)}, u32[]{:S(2)}, u32[]{:S(2)}) %collective-permute-start.2) | collective-permute-done | bytes 16416 | tf_op jit(solution)/shard_map/ppermute | solution.py:32
  20.8 0.1 pad_maximum_fusion.1
  20.8 0.0 copy-start.1
  20.8 0.1 broadcast_in_dim.14.param_ref
  20.9 7.9 %collective-permute-start.4 = (bf16[8,24,512]{2,1,0:T(8,128)(2,1)S(1)}, bf16[8,24,512]{2,1,0:T(8,128)(2,1)S(1)}, u32[]{:S(2)}, u32[]{:S(2)}) collective-permute-start(bf16[8,24,512]{2,1,0:T(8,128)(2,1)S(1)} %get-tuple-element.28), channel_id=1, source_target_pairs={{0,1},{1,2},{2,3},{3,4},{4,5},{5,6},{6,7},{7,8},{8,9},{9,10},{10,1... | collective-permute-start | bytes 589832 | tf_op jit(solution)/shard_map/ppermute | solution.py:26
  28.8 1.9 %collective-permute-start.5 = (bf16[8,24,512]{2,1,0:T(8,128)(2,1)S(1)}, bf16[8,24,512]{2,1,0:T(8,128)(2,1)S(1)}, u32[]{:S(2)}, u32[]{:S(2)}) collective-permute-start(bf16[8,24,512]{2,1,0:T(8,128)(2,1)S(1)} %get-tuple-element.29), channel_id=1, source_target_pairs={{1,0},{2,1},{3,2},{4,3},{5,4},{6,5},{7,6},{8,7},{9,8},{10,9},{11,1... | collective-permute-start | bytes 589832 | tf_op jit(solution)/shard_map/ppermute | solution.py:26
  30.8 0.0 collective-permute-done.above_ref
  30.8 0.0 collective-permute-done.1.below_ref
  30.8 1.0 %relay.1 = (bf16[8,64,512]{2,1,0:T(8,128)(2,1)S(1)}, bf16[8,64,512]{2,1,0:T(8,128)(2,1)S(1)}) custom-call(bf16[7,8,8,512]{3,2,1,0:T(8,128)(2,1)S(1)} %collective-permute-done.above_ref, bf16[7,8,8,512]{3,2,1,0:T(8,128)(2,1)S(1)} %collective-permute-done.1.below_ref), custom_call_target="tpu_custom_call" | custom-call | flops 1000000 | bytes 1966080 | tf_op jit(solution)/shard_map/relay/pallas_call | solution.py:369
  31.8 0.0 collective-permute-done.4.far_above_ref
  31.8 6.1 %collective-permute-done.5.far_below_ref = bf16[8,24,512]{2,1,0:T(8,128)(2,1)S(1)} collective-permute-done((bf16[8,24,512]{2,1,0:T(8,128)(2,1)S(1)}, bf16[8,24,512]{2,1,0:T(8,128)(2,1)S(1)}, u32[]{:S(2)}, u32[]{:S(2)}) %collective-permute-start.5) | collective-permute-done | bytes 196640 | tf_op jit(solution)/shard_map/ppermute | solution.py:26
  37.9 0.0 copy-done.1
  37.9 12.6 %track.1 = (f32[8,16,512]{2,1,0:T(8,128)S(1)}, f32[8,16,512]{2,1,0:T(8,128)S(1)}) custom-call(bf16[7,8,16,512]{3,2,1,0:T(8,128)(2,1)S(1)} %copy-done, bf16[7,8,8,512]{3,2,1,0:T(8,128)(2,1)S(1)} %collective-permute-done.above_ref, bf16[7,8,8,512]{3,2,1,0:T(8,128)(2,1)S(1)} %collective-permute-done.1.below_ref, ...), custom_call_target="tpu_custom_call" | custom-call | flops 40000000 | bytes 3330048 | tf_op jit(solution)/shard_map/track/pallas_call | solution.py:369
  50.6 9.6 %advect.1 = bf16[7,8,16,512]{3,2,1,0:T(8,128)(2,1)} custom-call(bf16[8,128,512]{2,1,0:T(8,128)(2,1)S(1)} %get-tuple-element.21.own_ref, bf16[8,64,512]{2,1,0:T(8,128)(2,1)S(1)} %get-tuple-element.30.above_ref, bf16[8,64,512]{2,1,0:T(8,128)(2,1)S(1)} %get-tuple-element.31.below_ref, bf16[8,8,128]{2,1,0:T(8,128)(2,1)S(1)} %collective-permute-done.2.west_ref, ...), custom_call_target="tpu_custom_call" | custom-call | flops 40000000 | bytes 4489216 | tf_op jit(solution)/shard_map/advect/pallas_call | solution.py:369
  (3 shorter events, 0.0 us)
Async XLA Ops:
  0.0 8.5 %copy-start = (bf16[7,8,16,512]{3,2,1,0:T(8,128)(2,1)S(1)}, bf16[7,8,16,512]{3,2,1,0:T(8,128)(2,1)}, u32[]{:S(2)}) copy-start(bf16[7,8,16,512]{3,2,1,0:T(8,128)(2,1)} %wind_ref.1) | copy-start | bytes 2752516
  1.3 29.4 %collective-permute-start = (bf16[7,8,8,512]{3,2,1,0:T(8,128)(2,1)S(1)}, bf16[7,8,8,512]{3,2,1,0:T(8,128)(2,1)S(1)}, u32[]{:S(2)}, u32[]{:S(2)}) collective-permute-start(bf16[7,8,8,512]{3,2,1,0:T(8,128)(2,1)S(1)} %get-tuple-element.38), channel_id=1, source_target_pairs={{0,1},{1,2},{2,3},{3,4},{4,5},{5,6},{6,7},{7,8},{8,9},{9,10},{10,1... | collective-permute-start | bytes 1376264 | tf_op jit(solution)/shard_map/ppermute | solution.py:26
  6.5 24.2 %collective-permute-start.1 = (bf16[7,8,8,512]{3,2,1,0:T(8,128)(2,1)S(1)}, bf16[7,8,8,512]{3,2,1,0:T(8,128)(2,1)S(1)}, u32[]{:S(2)}, u32[]{:S(2)}) collective-permute-start(bf16[7,8,8,512]{3,2,1,0:T(8,128)(2,1)S(1)} %get-tuple-element.37), channel_id=1, source_target_pairs={{1,0},{2,1},{3,2},{4,3},{5,4},{6,5},{7,6},{8,7},{9,8},{10,9},{11,1... | collective-permute-start | bytes 1376264 | tf_op jit(solution)/shard_map/ppermute | solution.py:26
  10.0 8.7 %collective-permute-start.3 = (bf16[8,8,128]{2,1,0:T(8,128)(2,1)S(1)}, bf16[8,8,128]{2,1,0:T(8,128)(2,1)S(1)}, u32[]{:S(2)}, u32[]{:S(2)}) collective-permute-start(bf16[8,8,128]{2,1,0:T(8,128)(2,1)S(1)} %get-tuple-element.26), channel_id=1, source_target_pairs={{0,224},{32,0},{64,32},{96,64},{128,96},{160,128},{192,160},{224,1... | collective-permute-start | bytes 49160 | tf_op jit(solution)/shard_map/ppermute | solution.py:32
  14.6 0.7 %copy-start.2 = (s32[2,1,1]{0,2,1:T(1,128)S(1)}, s32[2,1,1]{0,2,1:T(1,128)}, u32[]{:S(2)}) copy-start(s32[2,1,1]{0,2,1:T(1,128)} %param.4) | copy-start | bytes 28
  14.6 6.2 %collective-permute-start.2 = (bf16[8,8,128]{2,1,0:T(8,128)(2,1)S(1)}, bf16[8,8,128]{2,1,0:T(8,128)(2,1)S(1)}, u32[]{:S(2)}, u32[]{:S(2)}) collective-permute-start(bf16[8,8,128]{2,1,0:T(8,128)(2,1)S(1)} %get-tuple-element.25), channel_id=1, source_target_pairs={{0,32},{32,64},{64,96},{96,128},{128,160},{160,192},{192,224},{224... | collective-permute-start | bytes 49160 | tf_op jit(solution)/shard_map/ppermute | solution.py:32
  20.8 17.1 %copy-start.1 = (s32[2,8,16,512]{3,2,1,0:T(8,128)S(1)}, s32[2,8,16,512]{3,2,1,0:T(8,128)}, u32[]{:S(2)}) copy-start(s32[2,8,16,512]{3,2,1,0:T(8,128)} %cells_ref.3) | copy-start | bytes 1572868
  20.9 10.9 %collective-permute-start.4 = (bf16[8,24,512]{2,1,0:T(8,128)(2,1)S(1)}, bf16[8,24,512]{2,1,0:T(8,128)(2,1)S(1)}, u32[]{:S(2)}, u32[]{:S(2)}) collective-permute-start(bf16[8,24,512]{2,1,0:T(8,128)(2,1)S(1)} %get-tuple-element.28), channel_id=1, source_target_pairs={{0,1},{1,2},{2,3},{3,4},{4,5},{5,6},{6,7},{7,8},{8,9},{9,10},{10,1... | collective-permute-start | bytes 589832 | tf_op jit(solution)/shard_map/ppermute | solution.py:26
  28.8 9.1 %collective-permute-start.5 = (bf16[8,24,512]{2,1,0:T(8,128)(2,1)S(1)}, bf16[8,24,512]{2,1,0:T(8,128)(2,1)S(1)}, u32[]{:S(2)}, u32[]{:S(2)}) collective-permute-start(bf16[8,24,512]{2,1,0:T(8,128)(2,1)S(1)} %get-tuple-element.29), channel_id=1, source_target_pairs={{1,0},{2,1},{3,2},{4,3},{5,4},{6,5},{7,6},{8,7},{9,8},{10,9},{11,1... | collective-permute-start | bytes 589832 | tf_op jit(solution)/shard_map/ppermute | solution.py:26

commit v3 on v1

--- a/solution.py
+++ b/solution.py
@@ -378,7 +378,6 @@
     send_down, send_up, params = lax.optimization_barrier((send_down, send_up, params))
     far_above = passed_along(send_down, "lat", 1)
     far_below = passed_along(send_up, "lat", -1)
-    far_above, far_below, down, up = lax.optimization_barrier((far_above, far_below, down, up))
     above = passed_along(down, "lat", 1)
     below = passed_along(up, "lat", -1)
 
@@ -395,7 +394,7 @@
             pltpu.VMEM((tiles, 4 * 136, LANES), F32),
         ],
         [prognostic, far_above, far_below, west, east, cell_offsets, params],
-        "track", 40 * 10**6,
+        "track", 10**10,
     )
     return call(
         advect_kernel,

time: 55.3 us -> 52.6 us (0.951); the launches traced: 55 us -> 51.7 us
  waiting for transfers between devices: 12.1 us -> 5.71 us
  starting transfers between devices: 13.6 us -> 16.6 us
    ppermute x4, waiting for transfers between devices: 8.89 us -> 2.49 us  [passed_along(): return lax.ppermute(value, axis, pairs)]
    ppermute x4, starting transfers between devices: 10.7 us -> 13.7 us  [passed_along(): return lax.ppermute(value, axis, pairs)]
  transfers between devices with their start and end apart: 6 -> 6, of which waited for: 3 -> 2; matrix products, arithmetic and copies ran while one was open for 3% -> 3% of each run, Pallas kernels for 25% -> 27%
where the time goes in v3:
time: 52.6 us; the launch traced here: 51.7 us
  Pallas kernels  24.9 us (47%)
  starting transfers between devices  16.6 us (32%)
  waiting for transfers between devices  5.71 us (11%)
  local copies, waits for them, and re-layouts  2.68 us (5%)
  other arithmetic  0.92 us (2%)
  between operations  0.82 us (2%)
    pallas_call x4, Pallas kernels, call(): pl.pallas_call(kernel, in_specs=[in_vmem] * len(args), out_specs=[in_vmem...  24.9 us
    ppermute x4, starting transfers between devices, passed_along(): return lax.ppermute(value, axis, pairs)  13.7 us
    ppermute x2, waiting for transfers between devices, from_behind(): return lax.ppermute(value, axis, pairs)  3.22 us
    ppermute x2, starting transfers between devices, from_behind(): return lax.ppermute(value, axis, pairs)  2.91 us
    ppermute x4, waiting for transfers between devices, passed_along(): return lax.ppermute(value, axis, pairs)  2.49 us
    unnamed x8, local copies, waits for them, and re-layouts  1.84 us
  transfers between devices with their start and end apart: 6, of which 2 were waited for; matrix products, arithmetic and copies ran while one was open for 3% of the time, Pallas kernels for 27%

profile of v3, /device:TPU:135, one launch (start us, length us, event | category | flops | bytes accessed | tf_op | source)
XLA Modules:
  0.0 51.7 jit_solution(4989219420826843932)
XLA Ops:
  0.0 0.0 copy-start
  0.0 1.2 %copy-done = bf16[7,8,16,512]{3,2,1,0:T(8,128)(2,1)S(1)} copy-done((bf16[7,8,16,512]{3,2,1,0:T(8,128)(2,1)S(1)}, bf16[7,8,16,512]{3,2,1,0:T(8,128)(2,1)}, u32[]{:S(2)}) %copy-start) | copy-done | bytes 917528
  1.2 0.0 copy-start.1
  1.2 1.5 %edge.1 = (bf16[8,8,128]{2,1,0:T(8,128)(2,1)S(1)}, bf16[8,8,128]{2,1,0:T(8,128)(2,1)S(1)}) custom-call(bf16[7,8,16,512]{3,2,1,0:T(8,128)(2,1)S(1)} %copy-done), custom_call_target="tpu_custom_call" | custom-call | flops 1000000 | bytes 950272 | tf_op jit(solution)/shard_map/edge/pallas_call | solution.py:337
  2.7 2.9 %collective-permute-start.2 = (bf16[8,8,128]{2,1,0:T(8,128)(2,1)S(1)}, bf16[8,8,128]{2,1,0:T(8,128)(2,1)S(1)}, u32[]{:S(2)}, u32[]{:S(2)}) collective-permute-start(bf16[8,8,128]{2,1,0:T(8,128)(2,1)S(1)} %get-tuple-element.18), channel_id=1, source_target_pairs={{0,32},{32,64},{64,96},{96,128},{128,160},{160,192},{192,224},{224... | collective-permute-start | bytes 49160 | tf_op jit(solution)/shard_map/ppermute | solution.py:30
  5.6 0.0 collective-permute-start.3
  5.6 0.0 copy-start.3
  5.6 0.6 %copy-done.3 = s32[2,1,1]{0,2,1:T(1,128)S(1)} copy-done((s32[2,1,1]{0,2,1:T(1,128)S(1)}, s32[2,1,1]{0,2,1:T(1,128)}, u32[]{:S(2)}) %copy-start.3) | copy-done | bytes 32
  6.3 0.6 %fusion.1 = (f32[1,1,1]{0,2,1:T(1,128)}, f32[1,1,1]{0,2,1:T(1,128)}) fusion(f32[2,1,1]{0,2,1:T(1,128)S(1)} %get-tuple-element.33), kind=kLoop, calls=%fused_computation.12 | loop fusion | bytes 16 | tf_op jit(solution)/shard_map/slice | solution.py:371
  7.5 0.1 pad_maximum_fusion
  7.6 0.1 broadcast_in_dim.13
  7.7 0.1 reshape.15
  7.8 0.7 %multiply_divide_fusion = f32[16]{0:T(128)S(1)} fusion(f32[]{:T(128)} %bitcast.4, s32[]{:T(128)S(6)} %mul.12), kind=kLoop, calls=%fused_computation.9 | loop fusion | flops 112 | bytes 72 | tf_op jit(solution)/shard_map/div | solution.py:371
  8.5 0.1 pad_maximum_fusion.1
  8.6 0.0 collective-permute-done.2.west_ref
  8.6 3.2 %collective-permute-done.3.east_ref = bf16[8,8,128]{2,1,0:T(8,128)(2,1)S(1)} collective-permute-done((bf16[8,8,128]{2,1,0:T(8,128)(2,1)S(1)}, bf16[8,8,128]{2,1,0:T(8,128)(2,1)S(1)}, u32[]{:S(2)}, u32[]{:S(2)}) %collective-permute-start.3) | collective-permute-done | bytes 16416 | tf_op jit(solution)/shard_map/ppermute | solution.py:30
  11.8 0.1 maximum_maximum_fusion.2
  11.9 0.0 copy-start.2
  11.9 0.1 broadcast_in_dim.14.param_ref
  12.0 4.4 %collective-permute-start.4 = (bf16[8,24,512]{2,1,0:T(8,128)(2,1)S(1)}, bf16[8,24,512]{2,1,0:T(8,128)(2,1)S(1)}, u32[]{:S(2)}, u32[]{:S(2)}) collective-permute-start(bf16[8,24,512]{2,1,0:T(8,128)(2,1)S(1)} %get-tuple-element.20), channel_id=1, source_target_pairs={{0,1},{1,2},{2,3},{3,4},{4,5},{5,6},{6,7},{7,8},{8,9},{9,10},{10,1... | collective-permute-start | bytes 589832 | tf_op jit(solution)/shard_map/ppermute | solution.py:24
  16.4 1.9 %collective-permute-start.5 = (bf16[8,24,512]{2,1,0:T(8,128)(2,1)S(1)}, bf16[8,24,512]{2,1,0:T(8,128)(2,1)S(1)}, u32[]{:S(2)}, u32[]{:S(2)}) collective-permute-start(bf16[8,24,512]{2,1,0:T(8,128)(2,1)S(1)} %get-tuple-element.21), channel_id=1, source_target_pairs={{1,0},{2,1},{3,2},{4,3},{5,4},{6,5},{7,6},{8,7},{9,8},{10,9},{11,1... | collective-permute-start | bytes 589832 | tf_op jit(solution)/shard_map/ppermute | solution.py:24
  18.3 0.0 copy-done.1
  18.3 1.3 %pack.1 = (bf16[8,128,512]{2,1,0:T(8,128)(2,1)S(1)}, bf16[8,80,512]{2,1,0:T(8,128)(2,1)S(1)}, bf16[8,80,512]{2,1,0:T(8,128)(2,1)S(1)}) custom-call(bf16[7,8,16,512]{3,2,1,0:T(8,128)(2,1)S(1)} %copy-done.1), custom_call_target="tpu_custom_call" | custom-call | flops 1000000 | bytes 3276800 | tf_op jit(solution)/shard_map/pack/pallas_call | solution.py:337
  19.6 3.6 %collective-permute-start = (bf16[8,80,512]{2,1,0:T(8,128)(2,1)S(1)}, bf16[8,80,512]{2,1,0:T(8,128)(2,1)S(1)}, u32[]{:S(2)}, u32[]{:S(2)}) collective-permute-start(bf16[8,80,512]{2,1,0:T(8,128)(2,1)S(1)} %get-tuple-element.16), channel_id=1, source_target_pairs={{0,1},{1,2},{2,3},{3,4},{4,5},{5,6},{6,7},{7,8},{8,9},{9,10},{10,1... | collective-permute-start | bytes 1966088 | tf_op jit(solution)/shard_map/ppermute | solution.py:24
  23.3 3.7 %collective-permute-start.1 = (bf16[8,80,512]{2,1,0:T(8,128)(2,1)S(1)}, bf16[8,80,512]{2,1,0:T(8,128)(2,1)S(1)}, u32[]{:S(2)}, u32[]{:S(2)}) collective-permute-start(bf16[8,80,512]{2,1,0:T(8,128)(2,1)S(1)} %get-tuple-element.17), channel_id=1, source_target_pairs={{1,0},{2,1},{3,2},{4,3},{5,4},{6,5},{7,6},{8,7},{9,8},{10,9},{11,1... | collective-permute-start | bytes 1966088 | tf_op jit(solution)/shard_map/ppermute | solution.py:24
  27.0 0.0 collective-permute-done.4.above_ref.far_above_ref
  27.1 0.0 collective-permute-done.5.below_ref.far_below_ref
  27.1 0.0 copy-done.2
  27.1 12.6 %track.1 = (f32[8,16,512]{2,1,0:T(8,128)S(1)}, f32[8,16,512]{2,1,0:T(8,128)S(1)}) custom-call(bf16[7,8,16,512]{3,2,1,0:T(8,128)(2,1)S(1)} %copy-done.1, bf16[8,24,512]{2,1,0:T(8,128)(2,1)S(1)} %collective-permute-done.4.above_ref.far_above_ref, bf16[8,24,512]{2,1,0:T(8,128)(2,1)S(1)} %collective-permute-done.5.below_ref.far_below_ref, ...), custom_call_target="tpu_custom_call" | custom-call | flops 10000000000 | bytes 2412544 | tf_op jit(solution)/shard_map/track/pallas_call | solution.py:337
  39.7 0.0 collective-permute-done.above_ref
  39.7 2.5 %collective-permute-done.1.below_ref = bf16[8,80,512]{2,1,0:T(8,128)(2,1)S(1)} collective-permute-done((bf16[8,80,512]{2,1,0:T(8,128)(2,1)S(1)}, bf16[8,80,512]{2,1,0:T(8,128)(2,1)S(1)}, u32[]{:S(2)}, u32[]{:S(2)}) %collective-permute-start.1) | collective-permute-done | bytes 655392 | tf_op jit(solution)/shard_map/ppermute | solution.py:24
  42.2 9.4 %advect.1 = bf16[7,8,16,512]{3,2,1,0:T(8,128)(2,1)} custom-call(bf16[8,128,512]{2,1,0:T(8,128)(2,1)S(1)} %get-tuple-element.15.own_ref, bf16[8,80,512]{2,1,0:T(8,128)(2,1)S(1)} %collective-permute-done.above_ref, bf16[8,80,512]{2,1,0:T(8,128)(2,1)S(1)} %collective-permute-done.1.below_ref, bf16[8,8,128]{2,1,0:T(8,128)(2,1)S(1)} %collective-permute-done.2.west_ref, ...), custom_call_target="tpu_custom_call" | custom-call | flops 40000000 | bytes 4751360 | tf_op jit(solution)/shard_map/advect/pallas_call | solution.py:337
  (4 shorter events, 0.0 us)
Async XLA Ops:
  0.0 1.2 %copy-start = (bf16[7,8,16,512]{3,2,1,0:T(8,128)(2,1)S(1)}, bf16[7,8,16,512]{3,2,1,0:T(8,128)(2,1)}, u32[]{:S(2)}) copy-start(bf16[7,8,16,512]{3,2,1,0:T(8,128)(2,1)} %wind_ref.1) | copy-start | bytes 2752516
  1.2 17.1 %copy-start.1 = (bf16[7,8,16,512]{3,2,1,0:T(8,128)(2,1)S(1)}, bf16[7,8,16,512]{3,2,1,0:T(8,128)(2,1)}, u32[]{:S(2)}) copy-start(bf16[7,8,16,512]{3,2,1,0:T(8,128)(2,1)} %wind_ref.1) | copy-start | bytes 2752516
  2.7 5.9 %collective-permute-start.2 = (bf16[8,8,128]{2,1,0:T(8,128)(2,1)S(1)}, bf16[8,8,128]{2,1,0:T(8,128)(2,1)S(1)}, u32[]{:S(2)}, u32[]{:S(2)}) collective-permute-start(bf16[8,8,128]{2,1,0:T(8,128)(2,1)S(1)} %get-tuple-element.18), channel_id=1, source_target_pairs={{0,32},{32,64},{64,96},{96,128},{128,160},{160,192},{192,224},{224... | collective-permute-start | bytes 49160 | tf_op jit(solution)/shard_map/ppermute | solution.py:30
  5.6 6.2 %collective-permute-start.3 = (bf16[8,8,128]{2,1,0:T(8,128)(2,1)S(1)}, bf16[8,8,128]{2,1,0:T(8,128)(2,1)S(1)}, u32[]{:S(2)}, u32[]{:S(2)}) collective-permute-start(bf16[8,8,128]{2,1,0:T(8,128)(2,1)S(1)} %get-tuple-element.19), channel_id=1, source_target_pairs={{0,224},{32,0},{64,32},{96,64},{128,96},{160,128},{192,160},{224,1... | collective-permute-start | bytes 49160 | tf_op jit(solution)/shard_map/ppermute | solution.py:30
  5.6 0.7 %copy-start.3 = (s32[2,1,1]{0,2,1:T(1,128)S(1)}, s32[2,1,1]{0,2,1:T(1,128)}, u32[]{:S(2)}) copy-start(s32[2,1,1]{0,2,1:T(1,128)} %param.4) | copy-start | bytes 28
  11.9 15.2 %copy-start.2 = (s32[2,8,16,512]{3,2,1,0:T(8,128)S(1)}, s32[2,8,16,512]{3,2,1,0:T(8,128)}, u32[]{:S(2)}) copy-start(s32[2,8,16,512]{3,2,1,0:T(8,128)} %cells_ref.3) | copy-start | bytes 1572868
  12.0 15.1 %collective-permute-start.4 = (bf16[8,24,512]{2,1,0:T(8,128)(2,1)S(1)}, bf16[8,24,512]{2,1,0:T(8,128)(2,1)S(1)}, u32[]{:S(2)}, u32[]{:S(2)}) collective-permute-start(bf16[8,24,512]{2,1,0:T(8,128)(2,1)S(1)} %get-tuple-element.20), channel_id=1, source_target_pairs={{0,1},{1,2},{2,3},{3,4},{4,5},{5,6},{6,7},{7,8},{8,9},{9,10},{10,1... | collective-permute-start | bytes 589832 | tf_op jit(solution)/shard_map/ppermute | solution.py:24
  16.4 10.7 %collective-permute-start.5 = (bf16[8,24,512]{2,1,0:T(8,128)(2,1)S(1)}, bf16[8,24,512]{2,1,0:T(8,128)(2,1)S(1)}, u32[]{:S(2)}, u32[]{:S(2)}) collective-permute-start(bf16[8,24,512]{2,1,0:T(8,128)(2,1)S(1)} %get-tuple-element.21), channel_id=1, source_target_pairs={{1,0},{2,1},{3,2},{4,3},{5,4},{6,5},{7,6},{8,7},{9,8},{10,9},{11,1... | collective-permute-start | bytes 589832 | tf_op jit(solution)/shard_map/ppermute | solution.py:24
  19.6 20.1 %collective-permute-start = (bf16[8,80,512]{2,1,0:T(8,128)(2,1)S(1)}, bf16[8,80,512]{2,1,0:T(8,128)(2,1)S(1)}, u32[]{:S(2)}, u32[]{:S(2)}) collective-permute-start(bf16[8,80,512]{2,1,0:T(8,128)(2,1)S(1)} %get-tuple-element.16), channel_id=1, source_target_pairs={{0,1},{1,2},{2,3},{3,4},{4,5},{5,6},{6,7},{7,8},{8,9},{9,10},{10,1... | collective-permute-start | bytes 1966088 | tf_op jit(solution)/shard_map/ppermute | solution.py:24
  23.3 18.9 %collective-permute-start.1 = (bf16[8,80,512]{2,1,0:T(8,128)(2,1)S(1)}, bf16[8,80,512]{2,1,0:T(8,128)(2,1)S(1)}, u32[]{:S(2)}, u32[]{:S(2)}) collective-permute-start(bf16[8,80,512]{2,1,0:T(8,128)(2,1)S(1)} %get-tuple-element.17), channel_id=1, source_target_pairs={{1,0},{2,1},{3,2},{4,3},{5,4},{6,5},{7,6},{8,7},{9,8},{10,9},{11,1... | collective-permute-start | bytes 1966088 | tf_op jit(solution)/shard_map/ppermute | solution.py:24

commit v4 on v3

--- a/solution.py
+++ b/solution.py
@@ -12,6 +12,7 @@
 ITERS = 3
 WEST = 7
 LANES = 128
+SLOTS = 4
 F32 = jnp.float32
 BF16 = jnp.bfloat16
 
@@ -103,7 +104,7 @@
 def track_kernel(
     wind_ref, above_ref, below_ref, west_ref, east_ref, cells_ref, param_ref,
     row_frac_ref, col_frac_ref,
-    stage, spread, mask, lane_pos, dense, taps,
+    stages, spreads, mask, lane_pos, denses, tapss,
 ):
     _, levels, rows, cols = wind_ref.shape
     fill_band_tables(mask, lane_pos)
@@ -120,7 +121,10 @@
         lane = iota((16, LANES), 1)
         return jnp.where(lane < WEST, tall(west, 8), tall(east, 8 + WEST))[first : first + count]
 
-    def track_level(k, carry):
+    def prepare(k, slot):
+        stage = stages.at[slot]
+        spread = spreads.at[slot]
+        dense = denses.at[slot]
         lane = iota((32, LANES), 1)
         for c in range(2):
             above = above_ref[k, 8 * c : 8 * c + 8, :].astype(F32)
@@ -159,6 +163,10 @@
             dense[t, 0:16, :] = (col_mid[:, LANES * t : LANES * (t + 1)] + 6).astype(F32)
             dense[t, 16:32, :] = (row_mid[:, LANES * t : LANES * (t + 1)] + 4).astype(F32)
 
+    def collect(slot):
+        spread = spreads.at[slot]
+        dense = denses.at[slot]
+        taps = tapss.at[slot]
         def gather(pair, carry):
             y = 2 * pair
             start = pl.multiple_of(16 * pair + 16, 16)
@@ -192,8 +200,13 @@
                         taps[block, pl.ds(a * 136 + y + n, 8, stride=17), :] = v[a]
             return carry
 
-        lax.fori_loop(0, rows // 2, gather, 0, unroll=True)
-
+        for pair in range(rows // 2):
+            gather(pair, 0)
+
+    def iterate(k, slot):
+        taps = tapss.at[slot]
+        row_off = cells_ref[0, k]
+        col_off = cells_ref[1, k]
         for half in range(rows // 8):
             for tile in range(cols // LANES):
                 rr = slice(8 * half, 8 * half + 8)
@@ -231,21 +244,28 @@
                     fx = 0.5 + 0.5 * jnp.tanh(0.5 * (lx - oxf))
                 row_frac_ref[k, rr, cc] = fy
                 col_frac_ref[k, rr, cc] = fx
+
+    def track_levels(group, carry):
+        for slot in range(SLOTS):
+            prepare(SLOTS * group + slot, slot)
+        for slot in range(SLOTS):
+            collect(slot)
+            iterate(SLOTS * group + slot, slot)
         return carry
 
-    lax.fori_loop(0, levels, track_level, 0)
+    lax.fori_loop(0, levels // SLOTS, track_levels, 0)
 
 
 def advect_kernel(
     own_ref, above_ref, below_ref, west_ref, east_ref, far_above_ref, far_below_ref, cells_ref,
     row_frac_ref, col_frac_ref,
     out_ref,
-    spread, mask, lane_pos, dense, result,
+    spreads, mask, lane_pos, denses, results,
 ):
     channels, levels, rows, cols = out_ref.shape
     fill_band_tables(mask, lane_pos)
 
-    def place(block, west, east, first, count, at):
+    def place(spread, block, west, east, first, count, at):
         west = west.astype(F32)
         east = east.astype(F32)
         halo = []
@@ -261,10 +281,12 @@
         spread[at : at + 8 * count, LANES:cols] = block[:, LANES:]
         spread[at : at + 8 * count, cols:] = jnp.where(lanes < WEST, start, halo).astype(BF16)
 
-    def advect_level(k, carry):
-        place(above_ref[k], far_above_ref[k, 16:24, :LANES], far_above_ref[k, 16:24, LANES : 2 * LANES], rows - HL, HL, 0)
-        place(own_ref[k], west_ref[k], east_ref[k], 0, rows, 8 * HL)
-        place(below_ref[k], far_below_ref[k, 16:24, :LANES], far_below_ref[k, 16:24, LANES : 2 * LANES], 0, HL, 8 * (HL + rows))
+    def prepare(k, slot):
+        spread = spreads.at[slot]
+        dense = denses.at[slot]
+        place(spread, above_ref[k], far_above_ref[k, 16:24, :LANES], far_above_ref[k, 16:24, LANES : 2 * LANES], rows - HL, HL, 0)
+        place(spread, own_ref[k], west_ref[k], east_ref[k], 0, rows, 8 * HL)
+        place(spread, below_ref[k], far_below_ref[k, 16:24, :LANES], far_below_ref[k, 16:24, LANES : 2 * LANES], 0, HL, 8 * (HL + rows))
 
         for t in range(cols // LANES):
             cc = slice(LANES * t, LANES * (t + 1))
@@ -275,6 +297,10 @@
             for i, w in enumerate(cubic_weights(row_frac_ref[k, :, cc])):
                 dense[t, 96 + 16 * i : 112 + 16 * i, :] = w
 
+    def collect(k, slot):
+        spread = spreads.at[slot]
+        dense = denses.at[slot]
+        result = results.at[slot]
         def sample(pair, carry):
             y = 2 * pair
             start = pl.multiple_of(16 * pair, 16)
@@ -321,14 +347,21 @@
                     result[block, pl.ds(y + n, 8, stride=17), :] = total
             return carry
 
-        lax.fori_loop(0, rows // 2, sample, 0, unroll=True)
+        for pair in range(rows // 2):
+            sample(pair, 0)
         for c in range(channels):
             for t in range(cols // LANES):
                 cc = slice(LANES * t, LANES * (t + 1))
                 out_ref[c, k, :, cc] = result[t, 17 * c : 17 * c + 16, :].astype(BF16)
+
+    def advect_levels(group, carry):
+        for slot in range(SLOTS):
+            prepare(SLOTS * group + slot, slot)
+        for slot in range(SLOTS):
+            collect(SLOTS * group + slot, slot)
         return carry
 
-    lax.fori_loop(0, levels, advect_level, 0)
+    lax.fori_loop(0, levels // SLOTS, advect_levels, 0)
 
 
 def call(kernel, outs, scratch, args, name, flops):
@@ -386,12 +419,12 @@
         track_kernel,
         [frac, frac],
         [
-            pltpu.VMEM((tiles + 1, 8 * 32, LANES), F32),
-            pltpu.VMEM((8 * 32, cols + LANES), BF16),
+            pltpu.VMEM((SLOTS, tiles + 1, 8 * 32, LANES), F32),
+            pltpu.VMEM((SLOTS, 8 * 32, cols + LANES), BF16),
             pltpu.VMEM((144, 256), BF16),
             pltpu.VMEM((16, LANES), F32),
-            pltpu.VMEM((tiles, 32, LANES), F32),
-            pltpu.VMEM((tiles, 4 * 136, LANES), F32),
+            pltpu.VMEM((SLOTS, tiles, 32, LANES), F32),
+            pltpu.VMEM((SLOTS, tiles, 4 * 136, LANES), F32),
         ],
         [prognostic, far_above, far_below, west, east, cell_offsets, params],
         "track", 10**10,
@@ -400,11 +433,11 @@
         advect_kernel,
         [shape(prognostic.shape, BF16)],
         [
-            pltpu.VMEM((8 * (rows + 2 * HL), cols + LANES), BF16),
+            pltpu.VMEM((SLOTS, 8 * (rows + 2 * HL), cols + LANES), BF16),
             pltpu.VMEM((144, 256), BF16),
             pltpu.VMEM((16, LANES), F32),
-            pltpu.VMEM((tiles, 160, LANES), F32),
-            pltpu.VMEM((tiles, 136, LANES), F32),
+            pltpu.VMEM((SLOTS, tiles, 160, LANES), F32),
+            pltpu.VMEM((SLOTS, tiles, 136, LANES), F32),
         ],
         [own, above, below, west, east, far_above, far_below, cell_offsets, row_frac, col_frac],
         "advect", 40 * 10**6,

time: 52.6 us -> 51.4 us (0.977); the launches traced: 51.7 us -> 51.1 us
  Pallas kernels: 24.9 us -> 22.4 us
  waiting for transfers between devices: 5.71 us -> 7.68 us
    pallas_call x4, Pallas kernels: 24.9 us -> 22.4 us  [call(): pl.pallas_call(kernel, in_specs=[in_vmem] * len(args), out_specs=[in_vmem...]
    ppermute x4, waiting for transfers between devices: 2.49 us -> 4.46 us  [passed_along(): return lax.ppermute(value, axis, pairs)]
  transfers between devices with their start and end apart: 6 -> 6, of which waited for: 2 -> 3; matrix products, arithmetic and copies ran while one was open for 3% -> 3% of each run, Pallas kernels for 27% -> 23%
where the time goes in v4:
time: 51.4 us; the launch traced here: 51.1 us
  Pallas kernels  22.4 us (44%)
  starting transfers between devices  16.6 us (32%)
  waiting for transfers between devices  7.68 us (15%)
  local copies, waits for them, and re-layouts  2.68 us (5%)
  other arithmetic  0.92 us (2%)
  between operations  0.81 us (2%)
    pallas_call x4, Pallas kernels, call(): pl.pallas_call(kernel, in_specs=[in_vmem] * len(args), out_specs=[in_vmem...  22.4 us
    ppermute x4, starting transfers between devices, passed_along(): return lax.ppermute(value, axis, pairs)  13.7 us
    ppermute x4, waiting for transfers between devices, passed_along(): return lax.ppermute(value, axis, pairs)  4.46 us
    ppermute x2, waiting for transfers between devices, from_behind(): return lax.ppermute(value, axis, pairs)  3.22 us
    ppermute x2, starting transfers between devices, from_behind(): return lax.ppermute(value, axis, pairs)  2.91 us
    unnamed x8, local copies, waits for them, and re-layouts  1.84 us
  transfers between devices with their start and end apart: 6, of which 3 were waited for; matrix products, arithmetic and copies ran while one was open for 3% of the time, Pallas kernels for 23%

profile of v4, /device:TPU:135, one launch (start us, length us, event | category | flops | bytes accessed | tf_op | source)
XLA Modules:
  0.0 51.1 jit_solution(5693836231099233616)
XLA Ops:
  0.0 0.0 copy-start
  0.0 1.2 %copy-done = bf16[7,8,16,512]{3,2,1,0:T(8,128)(2,1)S(1)} copy-done((bf16[7,8,16,512]{3,2,1,0:T(8,128)(2,1)S(1)}, bf16[7,8,16,512]{3,2,1,0:T(8,128)(2,1)}, u32[]{:S(2)}) %copy-start) | copy-done | bytes 917528
  1.2 0.0 copy-start.1
  1.2 1.5 %edge.1 = (bf16[8,8,128]{2,1,0:T(8,128)(2,1)S(1)}, bf16[8,8,128]{2,1,0:T(8,128)(2,1)S(1)}) custom-call(bf16[7,8,16,512]{3,2,1,0:T(8,128)(2,1)S(1)} %copy-done), custom_call_target="tpu_custom_call" | custom-call | flops 1000000 | bytes 950272 | tf_op jit(solution)/shard_map/edge/pallas_call | solution.py:370
  2.7 2.9 %collective-permute-start.2 = (bf16[8,8,128]{2,1,0:T(8,128)(2,1)S(1)}, bf16[8,8,128]{2,1,0:T(8,128)(2,1)S(1)}, u32[]{:S(2)}, u32[]{:S(2)}) collective-permute-start(bf16[8,8,128]{2,1,0:T(8,128)(2,1)S(1)} %get-tuple-element.18), channel_id=1, source_target_pairs={{0,32},{32,64},{64,96},{96,128},{128,160},{160,192},{192,224},{224... | collective-permute-start | bytes 49160 | tf_op jit(solution)/shard_map/ppermute | solution.py:31
  5.6 0.0 collective-permute-start.3
  5.6 0.0 copy-start.3
  5.6 0.6 %copy-done.3 = s32[2,1,1]{0,2,1:T(1,128)S(1)} copy-done((s32[2,1,1]{0,2,1:T(1,128)S(1)}, s32[2,1,1]{0,2,1:T(1,128)}, u32[]{:S(2)}) %copy-start.3) | copy-done | bytes 32
  6.3 0.6 %fusion.1 = (f32[1,1,1]{0,2,1:T(1,128)}, f32[1,1,1]{0,2,1:T(1,128)}) fusion(f32[2,1,1]{0,2,1:T(1,128)S(1)} %get-tuple-element.33), kind=kLoop, calls=%fused_computation.12 | loop fusion | bytes 16 | tf_op jit(solution)/shard_map/slice | solution.py:404
  7.5 0.1 pad_maximum_fusion
  7.6 0.1 broadcast_in_dim.13
  7.7 0.1 reshape.15
  7.8 0.7 %multiply_divide_fusion = f32[16]{0:T(128)S(1)} fusion(f32[]{:T(128)} %bitcast.4, s32[]{:T(128)S(6)} %mul.12), kind=kLoop, calls=%fused_computation.9 | loop fusion | flops 112 | bytes 72 | tf_op jit(solution)/shard_map/div | solution.py:404
  8.5 0.1 pad_maximum_fusion.1
  8.6 0.0 collective-permute-done.2.west_ref
  8.6 3.2 %collective-permute-done.3.east_ref = bf16[8,8,128]{2,1,0:T(8,128)(2,1)S(1)} collective-permute-done((bf16[8,8,128]{2,1,0:T(8,128)(2,1)S(1)}, bf16[8,8,128]{2,1,0:T(8,128)(2,1)S(1)}, u32[]{:S(2)}, u32[]{:S(2)}) %collective-permute-start.3) | collective-permute-done | bytes 16416 | tf_op jit(solution)/shard_map/ppermute | solution.py:31
  11.8 0.1 maximum_maximum_fusion.2
  11.9 0.0 copy-start.2
  11.9 0.1 broadcast_in_dim.14.param_ref
  12.0 4.4 %collective-permute-start.4 = (bf16[8,24,512]{2,1,0:T(8,128)(2,1)S(1)}, bf16[8,24,512]{2,1,0:T(8,128)(2,1)S(1)}, u32[]{:S(2)}, u32[]{:S(2)}) collective-permute-start(bf16[8,24,512]{2,1,0:T(8,128)(2,1)S(1)} %get-tuple-element.20), channel_id=1, source_target_pairs={{0,1},{1,2},{2,3},{3,4},{4,5},{5,6},{6,7},{7,8},{8,9},{9,10},{10,1... | collective-permute-start | bytes 589832 | tf_op jit(solution)/shard_map/ppermute | solution.py:25
  16.4 1.9 %collective-permute-start.5 = (bf16[8,24,512]{2,1,0:T(8,128)(2,1)S(1)}, bf16[8,24,512]{2,1,0:T(8,128)(2,1)S(1)}, u32[]{:S(2)}, u32[]{:S(2)}) collective-permute-start(bf16[8,24,512]{2,1,0:T(8,128)(2,1)S(1)} %get-tuple-element.21), channel_id=1, source_target_pairs={{1,0},{2,1},{3,2},{4,3},{5,4},{6,5},{7,6},{8,7},{9,8},{10,9},{11,1... | collective-permute-start | bytes 589832 | tf_op jit(solution)/shard_map/ppermute | solution.py:25
  18.3 0.0 copy-done.1
  18.3 1.3 %pack.1 = (bf16[8,128,512]{2,1,0:T(8,128)(2,1)S(1)}, bf16[8,80,512]{2,1,0:T(8,128)(2,1)S(1)}, bf16[8,80,512]{2,1,0:T(8,128)(2,1)S(1)}) custom-call(bf16[7,8,16,512]{3,2,1,0:T(8,128)(2,1)S(1)} %copy-done.1), custom_call_target="tpu_custom_call" | custom-call | flops 1000000 | bytes 3276800 | tf_op jit(solution)/shard_map/pack/pallas_call | solution.py:370
  19.6 3.6 %collective-permute-start = (bf16[8,80,512]{2,1,0:T(8,128)(2,1)S(1)}, bf16[8,80,512]{2,1,0:T(8,128)(2,1)S(1)}, u32[]{:S(2)}, u32[]{:S(2)}) collective-permute-start(bf16[8,80,512]{2,1,0:T(8,128)(2,1)S(1)} %get-tuple-element.16), channel_id=1, source_target_pairs={{0,1},{1,2},{2,3},{3,4},{4,5},{5,6},{6,7},{7,8},{8,9},{9,10},{10,1... | collective-permute-start | bytes 1966088 | tf_op jit(solution)/shard_map/ppermute | solution.py:25
  23.3 3.7 %collective-permute-start.1 = (bf16[8,80,512]{2,1,0:T(8,128)(2,1)S(1)}, bf16[8,80,512]{2,1,0:T(8,128)(2,1)S(1)}, u32[]{:S(2)}, u32[]{:S(2)}) collective-permute-start(bf16[8,80,512]{2,1,0:T(8,128)(2,1)S(1)} %get-tuple-element.17), channel_id=1, source_target_pairs={{1,0},{2,1},{3,2},{4,3},{5,4},{6,5},{7,6},{8,7},{9,8},{10,9},{11,1... | collective-permute-start | bytes 1966088 | tf_op jit(solution)/shard_map/ppermute | solution.py:25
  27.0 0.0 collective-permute-done.4.above_ref.far_above_ref
  27.1 0.0 collective-permute-done.5.below_ref.far_below_ref
  27.1 0.0 copy-done.2
  27.1 10.7 %track.1 = (f32[8,16,512]{2,1,0:T(8,128)S(1)}, f32[8,16,512]{2,1,0:T(8,128)S(1)}) custom-call(bf16[7,8,16,512]{3,2,1,0:T(8,128)(2,1)S(1)} %copy-done.1, bf16[8,24,512]{2,1,0:T(8,128)(2,1)S(1)} %collective-permute-done.4.above_ref.far_above_ref, bf16[8,24,512]{2,1,0:T(8,128)(2,1)S(1)} %collective-permute-done.5.below_ref.far_below_ref, ...), custom_call_target="tpu_custom_call" | custom-call | flops 10000000000 | bytes 2412544 | tf_op jit(solution)/shard_map/track/pallas_call | solution.py:370
  37.8 0.2 collective-permute-done.above_ref
  37.9 4.3 %collective-permute-done.1.below_ref = bf16[8,80,512]{2,1,0:T(8,128)(2,1)S(1)} collective-permute-done((bf16[8,80,512]{2,1,0:T(8,128)(2,1)S(1)}, bf16[8,80,512]{2,1,0:T(8,128)(2,1)S(1)}, u32[]{:S(2)}, u32[]{:S(2)}) %collective-permute-start.1) | collective-permute-done | bytes 655392 | tf_op jit(solution)/shard_map/ppermute | solution.py:25
  42.2 8.9 %advect.1 = bf16[7,8,16,512]{3,2,1,0:T(8,128)(2,1)} custom-call(bf16[8,128,512]{2,1,0:T(8,128)(2,1)S(1)} %get-tuple-element.15.own_ref, bf16[8,80,512]{2,1,0:T(8,128)(2,1)S(1)} %collective-permute-done.above_ref, bf16[8,80,512]{2,1,0:T(8,128)(2,1)S(1)} %collective-permute-done.1.below_ref, bf16[8,8,128]{2,1,0:T(8,128)(2,1)S(1)} %collective-permute-done.2.west_ref, ...), custom_call_target="tpu_custom_call" | custom-call | flops 40000000 | bytes 4751360 | tf_op jit(solution)/shard_map/advect/pallas_call | solution.py:370
  (4 shorter events, 0.0 us)
Async XLA Ops:
  0.0 1.2 %copy-start = (bf16[7,8,16,512]{3,2,1,0:T(8,128)(2,1)S(1)}, bf16[7,8,16,512]{3,2,1,0:T(8,128)(2,1)}, u32[]{:S(2)}) copy-start(bf16[7,8,16,512]{3,2,1,0:T(8,128)(2,1)} %wind_ref.1) | copy-start | bytes 2752516
  1.2 17.1 %copy-start.1 = (bf16[7,8,16,512]{3,2,1,0:T(8,128)(2,1)S(1)}, bf16[7,8,16,512]{3,2,1,0:T(8,128)(2,1)}, u32[]{:S(2)}) copy-start(bf16[7,8,16,512]{3,2,1,0:T(8,128)(2,1)} %wind_ref.1) | copy-start | bytes 2752516
  2.7 5.9 %collective-permute-start.2 = (bf16[8,8,128]{2,1,0:T(8,128)(2,1)S(1)}, bf16[8,8,128]{2,1,0:T(8,128)(2,1)S(1)}, u32[]{:S(2)}, u32[]{:S(2)}) collective-permute-start(bf16[8,8,128]{2,1,0:T(8,128)(2,1)S(1)} %get-tuple-element.18), channel_id=1, source_target_pairs={{0,32},{32,64},{64,96},{96,128},{128,160},{160,192},{192,224},{224... | collective-permute-start | bytes 49160 | tf_op jit(solution)/shard_map/ppermute | solution.py:31
  5.6 6.2 %collective-permute-start.3 = (bf16[8,8,128]{2,1,0:T(8,128)(2,1)S(1)}, bf16[8,8,128]{2,1,0:T(8,128)(2,1)S(1)}, u32[]{:S(2)}, u32[]{:S(2)}) collective-permute-start(bf16[8,8,128]{2,1,0:T(8,128)(2,1)S(1)} %get-tuple-element.19), channel_id=1, source_target_pairs={{0,224},{32,0},{64,32},{96,64},{128,96},{160,128},{192,160},{224,1... | collective-permute-start | bytes 49160 | tf_op jit(solution)/shard_map/ppermute | solution.py:31
  5.6 0.7 %copy-start.3 = (s32[2,1,1]{0,2,1:T(1,128)S(1)}, s32[2,1,1]{0,2,1:T(1,128)}, u32[]{:S(2)}) copy-start(s32[2,1,1]{0,2,1:T(1,128)} %param.4) | copy-start | bytes 28
  11.9 15.2 %copy-start.2 = (s32[2,8,16,512]{3,2,1,0:T(8,128)S(1)}, s32[2,8,16,512]{3,2,1,0:T(8,128)}, u32[]{:S(2)}) copy-start(s32[2,8,16,512]{3,2,1,0:T(8,128)} %cells_ref.3) | copy-start | bytes 1572868
  12.0 15.1 %collective-permute-start.4 = (bf16[8,24,512]{2,1,0:T(8,128)(2,1)S(1)}, bf16[8,24,512]{2,1,0:T(8,128)(2,1)S(1)}, u32[]{:S(2)}, u32[]{:S(2)}) collective-permute-start(bf16[8,24,512]{2,1,0:T(8,128)(2,1)S(1)} %get-tuple-element.20), channel_id=1, source_target_pairs={{0,1},{1,2},{2,3},{3,4},{4,5},{5,6},{6,7},{7,8},{8,9},{9,10},{10,1... | collective-permute-start | bytes 589832 | tf_op jit(solution)/shard_map/ppermute | solution.py:25
  16.4 10.7 %collective-permute-start.5 = (bf16[8,24,512]{2,1,0:T(8,128)(2,1)S(1)}, bf16[8,24,512]{2,1,0:T(8,128)(2,1)S(1)}, u32[]{:S(2)}, u32[]{:S(2)}) collective-permute-start(bf16[8,24,512]{2,1,0:T(8,128)(2,1)S(1)} %get-tuple-element.21), channel_id=1, source_target_pairs={{1,0},{2,1},{3,2},{4,3},{5,4},{6,5},{7,6},{8,7},{9,8},{10,9},{11,1... | collective-permute-start | bytes 589832 | tf_op jit(solution)/shard_map/ppermute | solution.py:25
  19.6 18.3 %collective-permute-start = (bf16[8,80,512]{2,1,0:T(8,128)(2,1)S(1)}, bf16[8,80,512]{2,1,0:T(8,128)(2,1)S(1)}, u32[]{:S(2)}, u32[]{:S(2)}) collective-permute-start(bf16[8,80,512]{2,1,0:T(8,128)(2,1)S(1)} %get-tuple-element.16), channel_id=1, source_target_pairs={{0,1},{1,2},{2,3},{3,4},{4,5},{5,6},{6,7},{7,8},{8,9},{9,10},{10,1... | collective-permute-start | bytes 1966088 | tf_op jit(solution)/shard_map/ppermute | solution.py:25
  23.3 18.9 %collective-permute-start.1 = (bf16[8,80,512]{2,1,0:T(8,128)(2,1)S(1)}, bf16[8,80,512]{2,1,0:T(8,128)(2,1)S(1)}, u32[]{:S(2)}, u32[]{:S(2)}) collective-permute-start(bf16[8,80,512]{2,1,0:T(8,128)(2,1)S(1)} %get-tuple-element.17), channel_id=1, source_target_pairs={{1,0},{2,1},{3,2},{4,3},{5,4},{6,5},{7,6},{8,7},{9,8},{10,9},{11,1... | collective-permute-start | bytes 1966088 | tf_op jit(solution)/shard_map/ppermute | solution.py:25

commit v5 on v4

--- a/solution.py
+++ b/solution.py
@@ -102,12 +102,23 @@
 
 
 def track_kernel(
-    wind_ref, above_ref, below_ref, west_ref, east_ref, cells_ref, param_ref,
+    wind_ref, above_ref, below_ref, west_ref, east_ref, cells_ref, depth_ref,
     row_frac_ref, col_frac_ref,
-    stages, spreads, mask, lane_pos, denses, tapss,
+    stages, spreads, mask, lane_pos, denses, tapss, param_ref,
 ):
     _, levels, rows, cols = wind_ref.shape
     fill_band_tables(mask, lane_pos)
+    lat_total = rows * lax.axis_size("lat")
+    lat_index = (lax.axis_index("lat") * rows + iota((rows, LANES), 0)).astype(F32)
+    coslat = jnp.cos((lat_index + 0.5) * (math.pi / lat_total) - 0.5 * math.pi)
+    reach_y = jnp.full((8, LANES), depth_ref[0, 0, 0], jnp.int32).astype(F32) - 1.0
+    reach_x = jnp.full((8, LANES), depth_ref[1, 0, 0], jnp.int32).astype(F32) - 1.0
+    for half in range(rows // 8):
+        part = slice(8 * half, 8 * half + 8)
+        param_ref[part, :] = -courant / (coslat[part, :] * reach_x)
+    param_ref[16:24, :] = -courant / reach_y
+    param_ref[24:32, :] = reach_y
+    param_ref[32:40, :] = reach_x
 
     def edge(west, east, c, first, count):
         def tall(packed, shift):
@@ -369,7 +380,7 @@
     in_vmem = pl.BlockSpec(memory_space=pltpu.VMEM)
     return pl.pallas_call(
         kernel,
-        in_specs=[in_vmem] * len(args),
+        in_specs=[pl.BlockSpec(memory_space=pltpu.SMEM) if a.size == 2 else in_vmem for a in args],
         out_specs=[in_vmem] * len(outs),
         out_shape=outs,
         scratch_shapes=scratch,
@@ -396,19 +407,10 @@
         [prognostic], "pack", 10**6,
     )
 
-    lat_total = rows * lax.axis_size("lat")
-    lat_index = (lax.axis_index("lat") * rows + jnp.arange(rows, dtype=jnp.int32)).astype(F32)
-    coslat = jnp.cos((lat_index + 0.5) * (math.pi / lat_total) - 0.5 * math.pi)
-    reach = halo_depth[:, 0, 0].astype(F32) - 1.0
-    params = jnp.concatenate(
-        [-courant / (coslat * reach[1]), jnp.repeat(jnp.stack([-courant / reach[0], reach[0], reach[1]]), 8)]
-    )
-    params = jnp.broadcast_to(params[:, None], (rows + 24, LANES))
-
     edges = jnp.concatenate([west, east, jnp.zeros((levels, 8, cols - 2 * LANES), BF16)], axis=2)
     send_down = jnp.concatenate([prognostic[0, :, rows - 8 :], prognostic[1, :, rows - 8 :], edges], axis=1)
     send_up = jnp.concatenate([prognostic[0, :, :8], prognostic[1, :, :8], edges], axis=1)
-    send_down, send_up, params = lax.optimization_barrier((send_down, send_up, params))
+    send_down, send_up = lax.optimization_barrier((send_down, send_up))
     far_above = passed_along(send_down, "lat", 1)
     far_below = passed_along(send_up, "lat", -1)
     above = passed_along(down, "lat", 1)
@@ -425,8 +427,9 @@
             pltpu.VMEM((16, LANES), F32),
             pltpu.VMEM((SLOTS, tiles, 32, LANES), F32),
             pltpu.VMEM((SLOTS, tiles, 4 * 136, LANES), F32),
+            pltpu.VMEM((rows + 24, LANES), F32),
         ],
-        [prognostic, far_above, far_below, west, east, cell_offsets, params],
+        [prognostic, far_above, far_below, west, east, cell_offsets, halo_depth],
         "track", 10**10,
     )
     return call(

time: 51.4 us -> 55.1 us (1.072); the launches traced: 51.1 us -> 54 us
  Pallas kernels: 22.4 us -> 25.5 us
  waiting for transfers between devices: 7.68 us -> 8.58 us
  between operations: 0.81 us -> 0.11 us
    pallas_call x4, Pallas kernels: 22.4 us -> 25.5 us  [call(): pl.pallas_call(kernel, in_specs=[pl.BlockSpec(memory_space=pltpu.SMEM) if...]
    ppermute x2, waiting for transfers between devices: 3.22 us -> 6.14 us  [from_behind(): return lax.ppermute(value, axis, pairs)]
    ppermute x4, waiting for transfers between devices: 4.46 us -> 2.44 us  [passed_along(): return lax.ppermute(value, axis, pairs)]
    concatenate x1, other arithmetic: 0.07 us -> 0.83 us  [on_device(): jnp.concatenate([prognostic[0, :, :8], prognostic[1, :, :8], edges], axis=1)]
    div x1 -> x0, other arithmetic: 0.69 us -> none  [on_device(): -courant / (coslat * reach[1])]
    slice x1 -> x0, local copies, waits for them, and re-layouts: 0.59 us -> none  [on_device(): reach[1]]
    unnamed x8 -> x11, local copies, waits for them, and re-layouts: 1.84 us -> 2.32 us
  transfers between devices with their start and end apart: 6 -> 6, of which waited for: 3 -> 3; matrix products, arithmetic and copies ran while one was open for 3% -> 0% of each run, Pallas kernels for 23% -> 26%
where the time goes in v5:
time: 55.1 us; the launch traced here: 54 us
  Pallas kernels  25.5 us (46%)
  starting transfers between devices  16.6 us (30%)
  waiting for transfers between devices  8.58 us (16%)
  local copies, waits for them, and re-layouts  2.35 us (4%)
  other arithmetic  0.83 us (2%)
    pallas_call x4, Pallas kernels, call(): pl.pallas_call(kernel, in_specs=[pl.BlockSpec(memory_space=pltpu.SMEM) if...  25.5 us
    ppermute x4, starting transfers between devices, passed_along(): return lax.ppermute(value, axis, pairs)  13.7 us
    ppermute x2, waiting for transfers between devices, from_behind(): return lax.ppermute(value, axis, pairs)  6.14 us
    ppermute x2, starting transfers between devices, from_behind(): return lax.ppermute(value, axis, pairs)  2.91 us
    ppermute x4, waiting for transfers between devices, passed_along(): return lax.ppermute(value, axis, pairs)  2.44 us
    unnamed x11, local copies, waits for them, and re-layouts  2.32 us
  transfers between devices with their start and end apart: 6, of which 3 were waited for; matrix products, arithmetic and copies ran while one was open for 0% of the time, Pallas kernels for 26%

profile of v5, /device:TPU:135, one launch (start us, length us, event | category | flops | bytes accessed | tf_op | source)
XLA Modules:
  0.0 54.0 jit_solution(13917668293761281998)
XLA Ops:
  0.0 0.0 copy-start
  0.0 1.2 %copy-done = bf16[7,8,16,512]{3,2,1,0:T(8,128)(2,1)S(1)} copy-done((bf16[7,8,16,512]{3,2,1,0:T(8,128)(2,1)S(1)}, bf16[7,8,16,512]{3,2,1,0:T(8,128)(2,1)}, u32[]{:S(2)}) %copy-start) | copy-done | bytes 917528
  1.2 1.5 %edge.1 = (bf16[8,8,128]{2,1,0:T(8,128)(2,1)S(1)}, bf16[8,8,128]{2,1,0:T(8,128)(2,1)S(1)}) custom-call(bf16[7,8,16,512]{3,2,1,0:T(8,128)(2,1)S(1)} %copy-done), custom_call_target="tpu_custom_call" | custom-call | flops 1000000 | bytes 950272 | tf_op jit(solution)/shard_map/edge/pallas_call | solution.py:381
  2.7 2.9 %collective-permute-start.2 = (bf16[8,8,128]{2,1,0:T(8,128)(2,1)S(1)}, bf16[8,8,128]{2,1,0:T(8,128)(2,1)S(1)}, u32[]{:S(2)}, u32[]{:S(2)}) collective-permute-start(bf16[8,8,128]{2,1,0:T(8,128)(2,1)S(1)} %get-tuple-element.17), channel_id=1, source_target_pairs={{0,32},{32,64},{64,96},{96,128},{128,160},{160,192},{192,224},{224... | collective-permute-start | bytes 49160 | tf_op jit(solution)/shard_map/ppermute | solution.py:31
  5.6 0.0 collective-permute-start.3
  5.6 0.0 copy-start.1
  5.7 0.8 %collective-permute-done.2.west_ref = bf16[8,8,128]{2,1,0:T(8,128)(2,1)S(1)} collective-permute-done((bf16[8,8,128]{2,1,0:T(8,128)(2,1)S(1)}, bf16[8,8,128]{2,1,0:T(8,128)(2,1)S(1)}, u32[]{:S(2)}, u32[]{:S(2)}) %collective-permute-start.2) | collective-permute-done | bytes 16416 | tf_op jit(solution)/shard_map/ppermute | solution.py:31
  6.5 5.3 %collective-permute-done.3.east_ref = bf16[8,8,128]{2,1,0:T(8,128)(2,1)S(1)} collective-permute-done((bf16[8,8,128]{2,1,0:T(8,128)(2,1)S(1)}, bf16[8,8,128]{2,1,0:T(8,128)(2,1)S(1)}, u32[]{:S(2)}, u32[]{:S(2)}) %collective-permute-start.3) | collective-permute-done | bytes 16416 | tf_op jit(solution)/shard_map/ppermute | solution.py:31
  11.8 0.8 %maximum_maximum_fusion.2 = (bf16[8,24,512]{2,1,0:T(8,128)(2,1)}, bf16[8,24,512]{2,1,0:T(8,128)(2,1)}) fusion(bf16[8,8,512]{2,1,0:T(8,128)(2,1)S(1)} %get-tuple-element.26, bf16[8,8,512]{2,1,0:T(8,128)(2,1)S(1)} %get-tuple-element.23, bf16[8,8,128]{2,1,0:T(8,128)(2,1)S(1)} %collective-permute-done.3.east_ref, ...), kind=kLoop, calls=%fused_computation.2 | loop fusion | flops 1474560 | bytes 712704 | tf_op jit(solution)/shard_map/concatenate | solution.py:412
  12.6 4.3 %collective-permute-start.4 = (bf16[8,24,512]{2,1,0:T(8,128)(2,1)}, bf16[8,24,512]{2,1,0:T(8,128)(2,1)S(1)}, u32[]{:S(2)}, u32[]{:S(2)}) collective-permute-start(bf16[8,24,512]{2,1,0:T(8,128)(2,1)} %get-tuple-element.19), channel_id=1, source_target_pairs={{0,1},{1,2},{2,3},{3,4},{4,5},{5,6},{6,7},{7,8},{8,9},{9,10},{10,1... | collective-permute-start | bytes 589832 | tf_op jit(solution)/shard_map/ppermute | solution.py:25
  16.9 1.9 %collective-permute-start.5 = (bf16[8,24,512]{2,1,0:T(8,128)(2,1)}, bf16[8,24,512]{2,1,0:T(8,128)(2,1)}, u32[]{:S(2)}, u32[]{:S(2)}) collective-permute-start(bf16[8,24,512]{2,1,0:T(8,128)(2,1)} %get-tuple-element.20), channel_id=1, source_target_pairs={{1,0},{2,1},{3,2},{4,3},{5,4},{6,5},{7,6},{8,7},{9,8},{10,9},{11,1... | collective-permute-start | bytes 589832 | tf_op jit(solution)/shard_map/ppermute | solution.py:25
  18.8 2.4 %pack.1 = (bf16[8,128,512]{2,1,0:T(8,128)(2,1)S(1)}, bf16[8,80,512]{2,1,0:T(8,128)(2,1)}, bf16[8,80,512]{2,1,0:T(8,128)(2,1)}) custom-call(bf16[7,8,16,512]{3,2,1,0:T(8,128)(2,1)S(1)} %copy-done), custom_call_target="tpu_custom_call" | custom-call | flops 1000000 | bytes 3276800 | tf_op jit(solution)/shard_map/pack/pallas_call | solution.py:381
  21.2 0.0 copy-start.4
  21.2 3.8 %collective-permute-start = (bf16[8,80,512]{2,1,0:T(8,128)(2,1)}, bf16[8,80,512]{2,1,0:T(8,128)(2,1)S(1)}, u32[]{:S(2)}, u32[]{:S(2)}) collective-permute-start(bf16[8,80,512]{2,1,0:T(8,128)(2,1)} %get-tuple-element.15), channel_id=1, source_target_pairs={{0,1},{1,2},{2,3},{3,4},{4,5},{5,6},{6,7},{7,8},{8,9},{9,10},{10,1... | collective-permute-start | bytes 1966088 | tf_op jit(solution)/shard_map/ppermute | solution.py:25
  25.0 3.7 %collective-permute-start.1 = (bf16[8,80,512]{2,1,0:T(8,128)(2,1)}, bf16[8,80,512]{2,1,0:T(8,128)(2,1)S(1)}, u32[]{:S(2)}, u32[]{:S(2)}) collective-permute-start(bf16[8,80,512]{2,1,0:T(8,128)(2,1)} %get-tuple-element.16), channel_id=1, source_target_pairs={{1,0},{2,1},{3,2},{4,3},{5,4},{6,5},{7,6},{8,7},{9,8},{10,9},{11,1... | collective-permute-start | bytes 1966088 | tf_op jit(solution)/shard_map/ppermute | solution.py:25
  28.8 0.0 copy-done.4
  28.8 0.1 copy.4.depth_ref
  28.9 0.0 collective-permute-done.4.above_ref.far_above_ref
  28.9 0.0 collective-permute-done.5.below_ref.far_below_ref
  28.9 0.0 copy-done.1
  28.9 0.0 copy-start.2
  28.9 1.0 %copy-done.2 = s32[2,8,16,512]{3,2,1,0:T(8,128)S(1)} copy-done((s32[2,8,16,512]{3,2,1,0:T(8,128)S(1)}, s32[2,8,16,512]{3,2,1,0:T(8,128)}, u32[]{:S(2)}) %copy-start.2) | copy-done | bytes 524312
  29.9 0.0 copy-start.3
  29.9 11.8 %track.1 = (f32[8,16,512]{2,1,0:T(8,128)S(1)}, f32[8,16,512]{2,1,0:T(8,128)S(1)}) custom-call(bf16[7,8,16,512]{3,2,1,0:T(8,128)(2,1)S(1)} %copy-done.1, bf16[8,24,512]{2,1,0:T(8,128)(2,1)S(1)} %collective-permute-done.4.above_ref.far_above_ref, bf16[8,24,512]{2,1,0:T(8,128)(2,1)} %collective-permute-done.5.below_ref.far_below_ref, ...), custom_call_target="tpu_custom_call" | custom-call | flops 10000000000 | bytes 2392072 | tf_op jit(solution)/shard_map/track/pallas_call | solution.py:381
  41.7 0.0 collective-permute-done.above_ref
  41.7 2.4 %collective-permute-done.1.below_ref = bf16[8,80,512]{2,1,0:T(8,128)(2,1)S(1)} collective-permute-done((bf16[8,80,512]{2,1,0:T(8,128)(2,1)}, bf16[8,80,512]{2,1,0:T(8,128)(2,1)S(1)}, u32[]{:S(2)}, u32[]{:S(2)}) %collective-permute-start.1) | collective-permute-done | bytes 655392 | tf_op jit(solution)/shard_map/ppermute | solution.py:25
  44.1 0.0 copy-done.3
  44.1 9.9 %advect.1 = bf16[7,8,16,512]{3,2,1,0:T(8,128)(2,1)} custom-call(bf16[8,128,512]{2,1,0:T(8,128)(2,1)S(1)} %get-tuple-element.14.own_ref, bf16[8,80,512]{2,1,0:T(8,128)(2,1)S(1)} %collective-permute-done.above_ref, bf16[8,80,512]{2,1,0:T(8,128)(2,1)S(1)} %collective-permute-done.1.below_ref, bf16[8,8,128]{2,1,0:T(8,128)(2,1)S(1)} %collective-permute-done.2.west_ref, ...), custom_call_target="tpu_custom_call" | custom-call | flops 40000000 | bytes 4751360 | tf_op jit(solution)/shard_map/advect/pallas_call | solution.py:381
  (3 shorter events, 0.0 us)
Async XLA Ops:
  0.0 1.2 %copy-start = (bf16[7,8,16,512]{3,2,1,0:T(8,128)(2,1)S(1)}, bf16[7,8,16,512]{3,2,1,0:T(8,128)(2,1)}, u32[]{:S(2)}) copy-start(bf16[7,8,16,512]{3,2,1,0:T(8,128)(2,1)} %wind_ref.1) | copy-start | bytes 2752516
  2.7 3.8 %collective-permute-start.2 = (bf16[8,8,128]{2,1,0:T(8,128)(2,1)S(1)}, bf16[8,8,128]{2,1,0:T(8,128)(2,1)S(1)}, u32[]{:S(2)}, u32[]{:S(2)}) collective-permute-start(bf16[8,8,128]{2,1,0:T(8,128)(2,1)S(1)} %get-tuple-element.17), channel_id=1, source_target_pairs={{0,32},{32,64},{64,96},{96,128},{128,160},{160,192},{192,224},{224... | collective-permute-start | bytes 49160 | tf_op jit(solution)/shard_map/ppermute | solution.py:31
  5.6 6.2 %collective-permute-start.3 = (bf16[8,8,128]{2,1,0:T(8,128)(2,1)S(1)}, bf16[8,8,128]{2,1,0:T(8,128)(2,1)S(1)}, u32[]{:S(2)}, u32[]{:S(2)}) collective-permute-start(bf16[8,8,128]{2,1,0:T(8,128)(2,1)S(1)} %get-tuple-element.18), channel_id=1, source_target_pairs={{0,224},{32,0},{64,32},{96,64},{128,96},{160,128},{192,160},{224,1... | collective-permute-start | bytes 49160 | tf_op jit(solution)/shard_map/ppermute | solution.py:31
  5.6 23.2 %copy-start.1 = (bf16[7,8,16,512]{3,2,1,0:T(8,128)(2,1)S(1)}, bf16[7,8,16,512]{3,2,1,0:T(8,128)(2,1)}, u32[]{:S(2)}) copy-start(bf16[7,8,16,512]{3,2,1,0:T(8,128)(2,1)} %wind_ref.1) | copy-start | bytes 2752516
  12.6 16.2 %collective-permute-start.4 = (bf16[8,24,512]{2,1,0:T(8,128)(2,1)}, bf16[8,24,512]{2,1,0:T(8,128)(2,1)S(1)}, u32[]{:S(2)}, u32[]{:S(2)}) collective-permute-start(bf16[8,24,512]{2,1,0:T(8,128)(2,1)} %get-tuple-element.19), channel_id=1, source_target_pairs={{0,1},{1,2},{2,3},{3,4},{4,5},{5,6},{6,7},{7,8},{8,9},{9,10},{10,1... | collective-permute-start | bytes 589832 | tf_op jit(solution)/shard_map/ppermute | solution.py:25
  16.9 11.9 %collective-permute-start.5 = (bf16[8,24,512]{2,1,0:T(8,128)(2,1)}, bf16[8,24,512]{2,1,0:T(8,128)(2,1)}, u32[]{:S(2)}, u32[]{:S(2)}) collective-permute-start(bf16[8,24,512]{2,1,0:T(8,128)(2,1)} %get-tuple-element.20), channel_id=1, source_target_pairs={{1,0},{2,1},{3,2},{4,3},{5,4},{6,5},{7,6},{8,7},{9,8},{10,9},{11,1... | collective-permute-start | bytes 589832 | tf_op jit(solution)/shard_map/ppermute | solution.py:25
  21.2 7.5 %copy-start.4 = (s32[2,1,1]{0,2,1:T(1,128)S(1)}, s32[2,1,1]{0,2,1:T(1,128)}, u32[]{:S(2)}) copy-start(s32[2,1,1]{0,2,1:T(1,128)} %param.4) | copy-start | bytes 28
  21.2 20.5 %collective-permute-start = (bf16[8,80,512]{2,1,0:T(8,128)(2,1)}, bf16[8,80,512]{2,1,0:T(8,128)(2,1)S(1)}, u32[]{:S(2)}, u32[]{:S(2)}) collective-permute-start(bf16[8,80,512]{2,1,0:T(8,128)(2,1)} %get-tuple-element.15), channel_id=1, source_target_pairs={{0,1},{1,2},{2,3},{3,4},{4,5},{5,6},{6,7},{7,8},{8,9},{9,10},{10,1... | collective-permute-start | bytes 1966088 | tf_op jit(solution)/shard_map/ppermute | solution.py:25
  25.0 19.1 %collective-permute-start.1 = (bf16[8,80,512]{2,1,0:T(8,128)(2,1)}, bf16[8,80,512]{2,1,0:T(8,128)(2,1)S(1)}, u32[]{:S(2)}, u32[]{:S(2)}) collective-permute-start(bf16[8,80,512]{2,1,0:T(8,128)(2,1)} %get-tuple-element.16), channel_id=1, source_target_pairs={{1,0},{2,1},{3,2},{4,3},{5,4},{6,5},{7,6},{8,7},{9,8},{10,9},{11,1... | collective-permute-start | bytes 1966088 | tf_op jit(solution)/shard_map/ppermute | solution.py:25
  28.9 1.0 %copy-start.2 = (s32[2,8,16,512]{3,2,1,0:T(8,128)S(1)}, s32[2,8,16,512]{3,2,1,0:T(8,128)}, u32[]{:S(2)}) copy-start(s32[2,8,16,512]{3,2,1,0:T(8,128)} %cells_ref.3) | copy-start | bytes 1572868
  29.9 14.2 %copy-start.3 = (s32[2,8,16,512]{3,2,1,0:T(8,128)S(1)}, s32[2,8,16,512]{3,2,1,0:T(8,128)}, u32[]{:S(2)}) copy-start(s32[2,8,16,512]{3,2,1,0:T(8,128)} %cells_ref.3) | copy-start | bytes 1572868
